TPU v7x, 256 devices: a whole 4x4x8 slice. The times are simulated.
256 devices in a mesh: tile: 32 (over x, z), slide: 8 (over y, core).
Axes of the slice: x: 4, y: 4, z: 8, core: 2. Of those that a mesh axis runs over, the one named last changes fastest.
Arguments:
- tiles: bfloat16 [8, 96, 7, 7, 2048], P('slide', 'tile'), may hold values from -6 to 6
- tile_counts: int32 [8, 32], P('slide', 'tile'), may hold values from 1 to 3, as said below
- tile_weights: float32 [8, 96], P('slide', 'tile'), may hold values from 0.1 to 2
- slide_of: int32 [8, 96, 1], P('slide', 'tile'), may hold values from 0 to 31, as said below
- owner_map: int32 [8, 32], P('slide'), may hold values from 0 to 31, each once within a row
- cotangent: bfloat16 [8, 32, 2048], P('slide', 'tile'), may hold values from -6 to 6
- conv_weight: bfloat16 [9, 64, 2048], replicated, may hold values from -0.25 to 0.25
Outputs:
- pooled: float32 [8, 32, 2048], P('slide', 'tile')
- input_grads: float32 [8, 96, 7, 7, 2048], P('slide', 'tile')
- weight_grads: float32 [9, 64, 2048], P(None, None, 'tile')
Inputs may be any that keep to these rules, and one draw needn't show every extreme that they name: On every device the live tiles are the first tile_counts slots; in each slide group one device has all 3 slots live. `slide_of`: in each slide group, max(1, 8) slides name exactly one slot each, the first slot of some device; the other slots name the remaining slides evenly at random.
All inputs are finite; a program needn't handle non-finite values.
Results may differ from a plain program's by a relative error of at most 0.0065.
Values may be sent and summed in bfloat16 or wider, within the bound.
A program may use at most 128 MiB of HBM per device.

v0:
```python
import jax
import jax.numpy as jnp
from jax import lax
from jax.sharding import PartitionSpec as P

loss_scale = 512.0


def conv_forward(features, weight):
    count_rows, spatial = (features.shape[0], features.shape[1])
    group_width, channels = (weight.shape[1], weight.shape[2])
    groups = channels // group_width
    padded = jnp.pad(features, ((0, 0), (1, 1), (1, 1), (0, 0)))
    summed = jnp.zeros((count_rows, spatial, spatial, groups, group_width), jnp.float32)
    for offset in range(9):
        row_off, col_off = divmod(offset, 3)
        window = padded[:, row_off : row_off + spatial, col_off : col_off + spatial, :].reshape(
            count_rows, spatial, spatial, groups, group_width
        )
        tap = weight[offset].reshape(group_width, groups, group_width)
        summed = summed + jnp.einsum(
            "nhwgi,igo->nhwgo", window, tap, preferred_element_type=jnp.float32
        )
    return summed.reshape(count_rows, spatial, spatial, channels)


def conv_backward(features, weight, pre_grad):
    count_rows, spatial = (features.shape[0], features.shape[1])
    group_width, channels = (weight.shape[1], weight.shape[2])
    groups = channels // group_width
    padded = jnp.pad(features, ((0, 0), (1, 1), (1, 1), (0, 0)))
    grads_split = pre_grad.reshape(count_rows, spatial, spatial, groups, group_width)
    grads_padded = jnp.pad(grads_split, ((0, 0), (1, 1), (1, 1), (0, 0), (0, 0)))
    summed = jnp.zeros((count_rows, spatial, spatial, groups, group_width), jnp.float32)
    pieces = []
    for offset in range(9):
        row_off, col_off = divmod(offset, 3)
        window = padded[:, row_off : row_off + spatial, col_off : col_off + spatial, :].reshape(
            count_rows, spatial, spatial, groups, group_width
        )
        tap = weight[offset].reshape(group_width, groups, group_width)
        pieces.append(
            jnp.einsum(
                "nhwgi,nhwgo->igo", window, grads_split, preferred_element_type=jnp.float32
            ).reshape(group_width, channels)
        )
        shifted = grads_padded[
            :, 2 - row_off : 2 - row_off + spatial, 2 - col_off : 2 - col_off + spatial
        ]
        summed = summed + jnp.einsum(
            "nhwgo,igo->nhwgi", shifted, tap, preferred_element_type=jnp.float32
        )
    input_grads = summed.reshape(count_rows, spatial, spatial, channels)
    return (input_grads, jnp.stack(pieces, axis=0))


def shards(tiles, tile_counts, tile_weights, slide_of, owner_map, cotangent, conv_weight):
    features = tiles[0]
    slots = features.shape[0]
    spatial = features.shape[1]
    tile_total = lax.axis_size("tile")
    my_index = lax.axis_index("tile")
    alive = (jnp.arange(slots, dtype=jnp.int32) < tile_counts[0, 0]).astype(jnp.float32)
    tile_coef = alive * tile_weights[0]
    owner_ids = jnp.arange(tile_total, dtype=jnp.int32)
    slide_hits = slide_of[0, :, 0][:, None] == owner_ids[None, :]
    target = jnp.sum(jnp.where(slide_hits, owner_map[0][None, :], 0), axis=1)
    routing = (target[None, :] == owner_ids[:, None]).astype(jnp.float32) * tile_coef[None, :]
    pre = conv_forward(features, conv_weight)
    embedding = jnp.mean(jax.nn.silu(pre), axis=(1, 2)).astype(jnp.bfloat16)
    shares = lax.all_gather(routing, "tile", axis=1, tiled=True)
    own_row = lax.dynamic_slice_in_dim(shares, my_index, 1, 0)
    numerator = jnp.dot(
        own_row,
        lax.all_gather(embedding, "tile", axis=0, tiled=True).astype(jnp.float32),
        precision=lax.Precision.HIGHEST,
    )
    weight_total = jnp.sum(own_row, axis=1)
    denominator = jnp.maximum(weight_total, 1.0)
    pooled = numerator / denominator[:, None]
    scaled = (loss_scale * cotangent[0].astype(jnp.float32) / denominator[:, None]).astype(
        jnp.bfloat16
    )
    every_scaled = lax.all_gather(scaled, "tile", axis=0, tiled=True)
    tile_grads = jnp.dot(
        routing.T, every_scaled.astype(jnp.float32), precision=lax.Precision.HIGHEST
    )
    sigma = jax.nn.sigmoid(pre)
    slope = sigma * (1.0 + pre * (1.0 - sigma))
    pre_grad = (tile_grads[:, None, None, :] / (spatial * spatial) * slope).astype(jnp.bfloat16)
    input_grads, weight_terms = conv_backward(features, conv_weight, pre_grad)
    shard_sum = lax.psum_scatter(weight_terms, "tile", scatter_dimension=2, tiled=True)
    reduced = lax.psum(shard_sum, "slide")
    return (pooled[None], input_grads[None], reduced / loss_scale)


def solution(mesh):
    return jax.shard_map(
        shards,
        mesh=mesh,
        in_specs=(
            P("slide", "tile", None, None, None),
            P("slide", "tile"),
            P("slide", "tile"),
            P("slide", "tile", None),
            P("slide", None),
            P("slide", "tile", None),
            P(),
        ),
        out_specs=(
            P("slide", "tile", None),
            P("slide", "tile", None, None, None),
            P(None, None, "tile"),
        ),
        check_vma=False,
    )
```

profile of v0, /device:TPU:1, one launch (start us, length us, event | category | flops | bytes accessed | tf_op | source)
XLA Modules:
  0.0 546.1 jit_solution(8483302812085023196)
XLA Ops:
  9.5 40.3 %all-gather.1 = f32[32,3,32]{2,1,0:T(4,128)S(1)} all-gather(f32[1,3,32]{2,1,0:T(4,128)S(1)} %select_bitcast_fusion), channel_id=1, replica_groups=mesh['tile'=32,'slide'=8] {'tile'}, dimensions={0}, use_global_device_ids=true | all-gather | bytes 12672 | tf_op jit(solution)/shard_map/all_gather | solution.py:71
  51.9 36.1 %all-gather = bf16[32,1,2048]{2,1,0:T(2,128)(2,1)S(1)} all-gather(bf16[1,1,2048]{2,1,0:T(2,128)(2,1)S(1)} %divide_convert_fusion), channel_id=2, replica_groups=mesh['tile'=32,'slide'=8] {'tile'}, dimensions={0}, use_global_device_ids=true | all-gather | bytes 135168 | tf_op jit(solution)/shard_map/all_gather | solution.py:84
  103.6 2.8 pad_slice_fusion.12
  106.4 3.0 reshape.109
  117.4 3.3 reshape.113
  120.6 3.0 reshape.114
  123.6 3.2 reshape.106
  126.8 4.0 fusion.33
  139.1 2.9 fusion.38
  142.1 6.7 %multiply_convert_fusion = (bf16[3,7,7,32,64]{4,2,1,0,3:T(8,128)(2,1)S(1)}, f32[3,32,64]{2,0,1:T(4,128)S(1)}) fusion(f32[3,32,64]{2,0,1:T(4,128)S(1)} %copy.348, f32[32,3,7,7,64]{4,3,2,1,0:T(8,128)S(1)} %fusion.25, f32[32,3,7,7,64]{4,3,2,1,0:T(8,128)S(1)} %fusion.27, f32[32,3,7,7,64]{4,3,2,1,0:T(8,128)S(1)} %fusion.29, ...), kind=kOutput, calls=%fused_computation.22 | convolution fusion | flops 44249088 | bytes 11149312 | tf_op jit(solution)/shard_map/nhwgi,igo->nhwgo/dot_general | solution.py:21
  148.8 4.2 fusion.21
  153.0 2.4 fusion.19
  157.9 2.4 fusion.15
  160.3 2.4 fusion.13
  162.7 2.4 fusion.11
  165.1 2.6 fusion.9
  167.7 2.5 fusion.7
  199.8 12.9 %copy.450 = f32[9,64,2048]{1,0,2:T(8,128)} copy(f32[9,64,2048]{2,1,0:T(8,128)} %constant_dynamic-update-slice_fusion) | data formatting | bytes 9437184
  212.7 12.6 %reshape.153 = f32[2048,576]{1,0:T(8,128)} reshape(f32[2048,9,64]{2,1,0:T(8,128)} %bitcast.128) | data formatting | bytes 9437184
  225.5 34.7 %all-gather.2 = bf16[32,3,2048]{2,1,0:T(4,128)(2,1)S(1)} all-gather(bf16[1,3,2048]{2,1,0:T(4,128)(2,1)S(1)} %reshape.118), channel_id=1, replica_groups=mesh['tile'=32,'slide'=8] {'tile'}, dimensions={0}, use_global_device_ids=true | all-gather | bytes 405504 | tf_op jit(solution)/shard_map/all_gather | solution.py:75
  271.5 5.6 %add_bitcast_fusion = f32[3,7,7,32,64]{4,2,1,0,3:T(8,128)} fusion(f32[32,3,7,7,64]{4,3,2,1,0:T(8,128)S(1)} %fusion.6, f32[32,3,7,7,64]{4,3,2,1,0:T(8,128)S(1)} %fusion.5, f32[32,3,7,7,64]{4,3,2,1,0:T(8,128)S(1)} %fusion.4, f32[32,3,7,7,64]{4,3,2,1,0:T(8,128)} %fusion.50, f32[32,3,7,7,64]{4,3,2,1,0:T(8,128)S(1)} %fusion.3, ...), kind=kOutput, calls=%fused_computation.21 | convolution fusion | flops 40943616 | bytes 11702272 | tf_op jit(solution)/shard_map/nhwgo,igo->nhwgi/dot_general | solution.py:50
  277.1 192.1 %reduce-scatter.4.cloned.1.call-done = f32[64,576]{1,0:T(8,128)} async-done(((f32[2048,576]{1,0:T(8,128)}), f32[64,576]{1,0:T(8,128)}) %reduce-scatter.4.cloned.1.call-update) | async-done | bytes 147472
  474.0 2.5 broadcast_in_dim_reshape.4
  476.5 60.9 %all-reduce.4.cloned.1.call-done = f32[9,64,64]{2,1,0:T(8,128)} async-done(((f32[9,64,64]{2,1,0:T(8,128)}), f32[9,64,64]{2,1,0:T(8,128)}) %all-reduce.4.cloned.1.call-update) | async-done | bytes 147472 | tf_op jit(solution)/shard_map/psum | solution.py:93
  (135 shorter events, 84.4 us)
Async XLA Ops:
  7.2 81.2 %copy-start.23 = (bf16[1,3,7,7,2048]{4,3,2,1,0:T(8,128)(2,1)S(1)}, bf16[1,3,7,7,2048]{4,3,2,1,0:T(8,128)(2,1)}, u32[]{:S(2)}) copy-start(bf16[1,3,7,7,2048]{4,3,2,1,0:T(8,128)(2,1)} %param.7) | copy-start | bytes 1806340
  7.2 462.0 %reduce-scatter.4.cloned.1.call-start = ((), (), s32[]{:S(2)}) async-start(), calls=%async_computation.2 | async-start | bytes 5406720
  106.4 3.1 copy-start.24
  117.3 17.7 %copy-start = (bf16[3,7,7,32,64]{4,3,2,1,0:T(8,128)(2,1)}, bf16[3,7,7,32,64]{4,3,2,1,0:T(8,128)(2,1)S(1)}, u32[]{:S(2)}) copy-start(bf16[3,7,7,32,64]{4,3,2,1,0:T(8,128)(2,1)S(1)} %reshape.112) | copy-start | bytes 1806340
  126.8 4.0 copy-start.4
  126.8 4.0 copy-start.15
  130.8 1.4 copy-start.3
  130.8 1.4 copy-start.13
  132.2 1.4 copy-start.2
  132.2 1.4 copy-start.19
  137.7 1.4 copy-start.21
  148.8 4.2 copy-start.8
  153.0 2.5 copy-start.9
  155.4 2.4 copy-start.31
  160.3 2.4 copy-start.1
  167.7 2.5 copy-start.5
  190.0 3.9 copy-start.30
  190.0 4.8 copy-start.29
  192.0 3.6 copy-start.28
  193.9 2.5 copy-start.27
  194.8 2.5 copy-start.26
  225.3 35.5 %copy-start.22 = (bf16[64,32,64]{2,1,0:T(8,128)(2,1)S(1)}, bf16[64,32,64]{2,1,0:T(8,128)(2,1)}, u32[]{:S(2)}) copy-start(bf16[64,32,64]{2,1,0:T(8,128)(2,1)} %reshape_squeeze.37) | copy-start | bytes 786436
  225.3 312.1 %all-reduce.4.cloned.1.call-start = ((), (), s32[]{:S(2)}) async-start(), calls=%async_computation.1 | async-start | bytes 589824 | tf_op jit(solution)/shard_map/psum | solution.py:93
  269.1 2.4 copy-start.14
  (10 other events, 12.4 us)
Sparse Core Ops, SparseCore 0:
  225.4 243.7 reduce-scatter.3
  472.1 65.2 all-reduce.3
where the time goes:
time: 554 us; the launch traced here: 546 us
  waiting for transfers between devices  253 us (46%)
  blocking collectives  111 us (20%)
  local copies, waits for them, and re-layouts  99.6 us (18%)
  matrix products  61 us (11%)
  between operations  16 us (3%)
    unnamed x3, waiting for transfers between devices  192 us
    psum x1, waiting for transfers between devices, shards(): reduced = lax.psum(shard_sum, 'slide')  60.9 us
    all_gather x1, blocking collectives, shards(): shares = lax.all_gather(routing, 'tile', axis=1, tiled=True)  40.3 us
    unnamed x79, local copies, waits for them, and re-layouts  37.2 us
    all_gather x1, blocking collectives, shards(): every_scaled = lax.all_gather(scaled, 'tile', axis=0, tiled=True)  36.1 us
    all_gather x1, blocking collectives, shards(): lax.all_gather(embedding, 'tile', axis=0, tiled=True).astype(jnp.float32)  34.7 us
    dot_general x9, matrix products, conv_backward(): jnp.einsum('nhwgi,nhwgo->igo', window, grads_split, preferred_element_typ...  22.9 us
    reshape x9, local copies, waits for them, and re-layouts, conv_forward(): padded[:, row_off:row_off + spatial, col_off:col_off + spatial, :]  22.6 us
  transfers between devices with their start and end apart: 2, of which 2 were waited for; matrix products, arithmetic and copies ran while one was open for 4% of the time, Pallas kernels for 0%

commit v1 on v0

v1 whole, which is shorter than its diff:
```python
import functools

import jax
import jax.numpy as jnp
from jax import lax
from jax.experimental import pallas as pl
from jax.experimental.pallas import tpu as pltpu
from jax.sharding import PartitionSpec as P

MESH = pl.DeviceIdType.MESH
LOSS_SCALE = 512.0
SIDE = 7
SLOTS = 3
WIDTH = 64
LANES = 128
TAPS = 9
ROWS = SLOTS * 64
BASE = 16
PADDED = BASE + ROWS + 16
PACKED = TAPS * WIDTH // 2
f32 = jnp.float32
bf16 = jnp.bfloat16


class Sizes:
    def __init__(self, mesh):
        self.tiles = mesh.shape["tile"]
        self.slides = mesh.shape["slide"]
        self.ny = self.slides // 2
        self.nx = self.ny
        self.nz = self.tiles // self.nx
        self.pairs = self.tiles // 2
        self.piece = PACKED // self.nz


def position(sz):
    tile = lax.axis_index("tile")
    slide = lax.axis_index("slide")
    return tile, slide, tile // sz.nz, tile % sz.nz, slide // 2, slide % 2


def remote(src, dst, send, recv, device):
    return pltpu.make_async_remote_copy(
        src_ref=src, dst_ref=dst, send_sem=send, recv_sem=recv, device_id=device, device_id_type=MESH
    )


def signal(device):
    pl.semaphore_signal(pltpu.get_barrier_semaphore(), inc=1, device_id=device, device_id_type=MESH)


def slot_route(slot, counts, weights, slide_of, owner_map):
    coef = jnp.where(slot < counts[0, 0], weights[0, slot], 0.0)
    return coef, owner_map[0, slide_of[0, slot, 0]]


def gather_kernel(
    sz, counts, weights, slide_of, owner_map, cot, grad_out, den_out,
    stage, all_cot, my_total, z_total, x_total, total, zs, zr, xs, xr, tzs, tzr, txs, txr,
):
    tile, slide, x, z, y, c = position(sz)
    z_peers = [(x * sz.nz + (z + off) % sz.nz, slide) for off in range(1, sz.nz)]
    x_peers = [(((x + off) % sz.nx) * sz.nz + z, slide) for off in range(1, sz.nx)]
    for peer in z_peers + x_peers:
        signal(peer)
    for j in range(sz.pairs):
        stage[pl.ds(j, 1), :] = cot[0, :, pl.ds(j * LANES, LANES)].astype(f32)
    all_cot[tile] = stage[...].astype(bf16)
    lane = lax.broadcasted_iota(jnp.int32, (8, LANES), 1)
    routes = [slot_route(s, counts, weights, slide_of, owner_map) for s in range(SLOTS)]
    mine = jnp.zeros((8, LANES), f32)
    for coef, target in routes:
        mine = mine + jnp.where(lane == target, coef, 0.0)
    my_total[...] = mine
    pl.semaphore_wait(pltpu.get_barrier_semaphore(), len(z_peers) + len(x_peers))

    copies = []
    for i, peer in enumerate(z_peers):
        copies.append(remote(my_total, z_total.at[i], tzs.at[i], tzr.at[i], peer))
        copies.append(remote(all_cot.at[tile], all_cot.at[tile], zs.at[i], zr.at[i], peer))
    for copy in copies:
        copy.start()
    for i in range(sz.nz - 1):
        source = x * sz.nz + (z + sz.nz - 1 - i) % sz.nz
        remote(my_total, z_total.at[i], tzs.at[i], tzr.at[i], z_peers[i]).wait_recv()
        remote(all_cot.at[tile], all_cot.at[source], zs.at[i], zr.at[i], z_peers[i]).wait_recv()
        mine = mine + z_total[i]
    total[...] = mine
    later = []
    for i, peer in enumerate(x_peers):
        block = all_cot.at[pl.ds(x * sz.nz, sz.nz)]
        later.append(remote(total, x_total.at[i], txs.at[i], txr.at[i], peer))
        later.append(remote(block, block, xs.at[i], xr.at[i], peer))
    for copy in later:
        copy.start()
    for i in range(sz.nx - 1):
        source = (x + sz.nx - 1 - i) % sz.nx
        remote(total, x_total.at[i], txs.at[i], txr.at[i], x_peers[i]).wait_recv()
        block = all_cot.at[pl.ds(source * sz.nz, sz.nz)]
        remote(block, block, xs.at[i], xr.at[i], x_peers[i]).wait_recv()
        mine = mine + x_total[i]
    for copy in copies + later:
        copy.wait_send()

    denominator = jnp.maximum(mine, 1.0)

    def pick(owner):
        found = jnp.sum(jnp.where(lane == owner, denominator, 0.0), axis=1, keepdims=True)
        return jnp.broadcast_to(found[0:1], (sz.pairs, LANES))

    den_out[...] = pick(tile)
    for s, (coef, target) in enumerate(routes):
        scaled = (LOSS_SCALE * all_cot[target].astype(f32) / pick(target)).astype(bf16)
        grad_out[s] = coef * scaled.astype(f32)


def compute_kernel(
    sz, counts, weights, slide_of, owner_map, tiles, weight, grad, input_grad, terms, parts,
    xp, gp, xc, gc, w_rows, w_lanes,
):
    pair = pl.program_id(0)

    @pl.when(pair == 0)
    def _():
        xp[...] = jnp.zeros_like(xp)
        gp[...] = jnp.zeros_like(gp)

    low = lax.broadcasted_iota(jnp.int32, (WIDTH, LANES), 1) < WIDTH
    for tap in range(TAPS):
        w = weight[tap]
        zero = jnp.zeros_like(w)
        first, second = jnp.where(low, w, zero), jnp.where(low, zero, w)
        w_rows[pl.ds(tap * LANES, WIDTH), :] = first
        w_rows[pl.ds(tap * LANES + WIDTH, WIDTH), :] = second
        w_lanes[pl.ds(0, WIDTH), pl.ds(tap * LANES, LANES)] = first
        w_lanes[pl.ds(WIDTH, WIDTH), pl.ds(tap * LANES, LANES)] = second
    for t in range(SLOTS):
        for h in range(SIDE):
            xp[pl.ds(BASE + 64 * t + 8 * h, SIDE), :] = tiles[0, t, h].astype(f32)
    for tap in range(TAPS):
        shift = 8 * (tap // 3 - 1) + tap % 3 - 1
        xc[:, pl.ds(tap * LANES, LANES)] = xp[pl.ds(BASE + shift, ROWS), :].astype(bf16)
    pre = jnp.dot(xc[...], w_rows[...], preferred_element_type=f32)
    sigma = 1.0 / (1.0 + jnp.exp(-pre))
    row = lax.broadcasted_iota(jnp.int32, (64, LANES), 0)
    real = (row % 8 < SIDE) & (row < 8 * SIDE)
    owner = lax.broadcasted_iota(jnp.int32, (sz.tiles, LANES), 0)
    part = jnp.zeros((sz.tiles, LANES), f32)
    pieces = []
    for t in range(SLOTS):
        v, q = pre[64 * t : 64 * t + 64], sigma[64 * t : 64 * t + 64]
        mean = jnp.sum(jnp.where(real, v * q, 0.0), axis=0, keepdims=True) / (SIDE * SIDE)
        embedding = mean.astype(bf16).astype(f32)
        coef, target = slot_route(t, counts, weights, slide_of, owner_map)
        part = part + jnp.where(owner == target, coef, 0.0) * embedding
        slope = q * (1.0 + v * (1.0 - q))
        upstream = grad[t, pl.ds(pair, 1), :] / (SIDE * SIDE)
        pieces.append(jnp.where(real, upstream * slope, 0.0))
    parts[:, pl.ds(pair, 1), :] = part.reshape(sz.tiles, 1, LANES)
    g = jnp.concatenate(pieces, axis=0)
    gp[pl.ds(BASE, ROWS), :] = g
    for tap in range(TAPS):
        shift = 8 * (tap // 3 - 1) + tap % 3 - 1
        gc[:, pl.ds(tap * LANES, LANES)] = gp[pl.ds(BASE - shift, ROWS), :].astype(bf16)
    dx = lax.dot_general(gc[...], w_lanes[...], (((1,), (1,)), ((), ())), preferred_element_type=f32)
    for t in range(SLOTS):
        for h in range(SIDE):
            at = 64 * t + 8 * h
            input_grad[0, t, h] = dx[at : at + SIDE]
    dw = jnp.dot(g.astype(bf16).T, xc[...], preferred_element_type=f32)
    low = lax.broadcasted_iota(jnp.int32, (32, LANES), 1) < WIDTH
    for tap in range(TAPS):
        d = dw[:, tap * LANES : (tap + 1) * LANES]
        even = jnp.where(low, d[0:32], pltpu.roll(d[32:64], WIDTH, 1))
        odd = jnp.where(low, pltpu.roll(d[64:96], WIDTH, 1), d[96:128])
        terms[0, 0, pl.ds(tap * 32, 32), :] = even.astype(bf16)
        terms[1, 0, pl.ds(tap * 32, 32), :] = odd.astype(bf16)


def reduce_kernel(
    sz, terms, parts, den, pooled, result,
    c_in, s1, y_in, s2, x_in, s3f, s3, z_in, own, fin, px_in, psum, pz_in,
    cs, cr, ys, yr, xs, xr, zs, zr, fs, fr, pxs, pxr, pzs, pzr,
):
    tile, slide, x, z, y, c = position(sz)
    nx, ny, nz = sz.nx, sz.ny, sz.nz
    mate = (tile, y * 2 + 1 - c)
    y_peers = [(tile, ((y + off) % ny) * 2 + c) for off in range(1, ny)]
    x_peers = [(((x + off) % nx) * nz + z, slide) for off in range(1, nx)]
    z_peers = [(x * nz + (z + off) % nz, slide) for off in range(1, nz)]
    home = y * nz + 2 * x + c
    at_home = home == tile
    homes = [(home, (slide + d) % sz.slides) for d in range(sz.slides)]
    source_slide = x * 2 + z % 2
    sources = [((z // 2) * nz + q, source_slide) for q in range(nz)]
    symmetric = [mate] + y_peers + x_peers + z_peers
    for peer in symmetric:
        signal(peer)
    for q in range(nz):

        @pl.when(jnp.logical_not(at_home & (z == q)))
        def _():
            signal(sources[q])

    pl.semaphore_wait(
        pltpu.get_barrier_semaphore(), len(symmetric) + sz.slides - at_home.astype(jnp.int32)
    )
    started = []

    def start(copy):
        copy.start()
        started.append(copy)
        return copy

    p_copies = []
    for i, peer in enumerate(x_peers):
        xo = (x + i + 1) % nx
        p_copies.append(start(remote(parts.at[pl.ds(xo * nz, nz)], px_in.at[i], pxs.at[i], pxr.at[i], peer)))
    order = list(range(1, ny)) + [0]
    c_copies = []
    for i, off in enumerate(order):
        block = pl.ds(((y + off) % ny) * nx, nx)
        c_copies.append(start(remote(terms.at[1 - c, block], c_in.at[block], cs.at[i], cr.at[i], mate)))
    y_copies = []
    for i, off in enumerate(order):
        first = ((y + off) % ny) * nx
        c_copies[i].wait_recv()

        @pl.loop(0, nx)
        def _(k):
            s1[first + k] = (terms[c, first + k].astype(f32) + c_in[first + k].astype(f32)).astype(bf16)

        if off:
            y_copies.append(start(remote(s1.at[pl.ds(first, nx)], y_in.at[off - 1], ys.at[off - 1], yr.at[off - 1], y_peers[off - 1])))
    for copy in p_copies:
        copy.wait_recv()

    @pl.loop(0, nz)
    def _(k):
        v = parts[x * nz + k]
        for i in range(nx - 1):
            v = v + px_in[i, k]
        psum[k] = v

    pz_copies = []
    for i, peer in enumerate(z_peers):
        pz_copies.append(start(remote(psum.at[(z + i + 1) % nz], pz_in.at[i], pzs.at[i], pzr.at[i], peer)))
    for copy in y_copies:
        copy.wait_recv()

    @pl.loop(0, nx)
    def _(k):
        v = s1[y * nx + k].astype(f32)
        for i in range(ny - 1):
            v = v + y_in[i, k].astype(f32)
        s2[k] = v.astype(bf16)

    x_copies = []
    for i, peer in enumerate(x_peers):
        x_copies.append(start(remote(s2.at[(x + i + 1) % nx], x_in.at[i], xs.at[i], xr.at[i], peer)))
    for copy in x_copies:
        copy.wait_recv()
    v = s2[x].astype(f32)
    for i in range(nx - 1):
        v = v + x_in[i].astype(f32)
    s3f[...] = v
    for q in range(nz):
        s3[q, pl.ds(0, sz.piece), :] = s3f[pl.ds(q * sz.piece, sz.piece), :].astype(bf16)
    z_copies = []
    for i, peer in enumerate(z_peers):
        z_copies.append(start(remote(s3.at[(z + i + 1) % nz], z_in.at[i], zs.at[i], zr.at[i], peer)))
    for copy in z_copies:
        copy.wait_recv()
    v = s3[z, pl.ds(0, sz.piece), :].astype(f32)
    for i in range(nz - 1):
        v = v + z_in[i, pl.ds(0, sz.piece), :].astype(f32)
    own[pl.ds(0, sz.piece), :] = v / LOSS_SCALE
    for d, peer in enumerate(homes):
        copy = remote(own, fin.at[z], fs.at[d], fr.at[z], peer)
        if d == 0:

            @pl.when(jnp.logical_not(at_home))
            def _():
                copy.start()

        else:
            start(copy)

    @pl.when(at_home)
    def _():
        fin[z] = own[...]

    for copy in pz_copies:
        copy.wait_recv()
    v = psum[z]
    for i in range(nz - 1):
        v = v + pz_in[i]
    pooled[...] = v / den[...]
    for q in range(nz):

        @pl.when(jnp.logical_not(at_home & (z == q)))
        def _():
            remote(own, fin.at[q], fs.at[0], fr.at[q], sources[q]).wait_recv()

    for q in range(nz):
        result[pl.ds(q * sz.piece, sz.piece), :] = fin[q, pl.ds(0, sz.piece), :]

    @pl.when(jnp.logical_not(at_home))
    def _():
        remote(own, fin.at[z], fs.at[0], fr.at[z], homes[0]).wait_send()

    for copy in started:
        copy.wait_send()


def shards(sz, tiles, counts, weights, slide_of, owner_map, cot, conv_weight):
    pairs, channels = sz.pairs, sz.tiles * WIDTH
    smem = pl.BlockSpec(memory_space=pltpu.SMEM)
    vmem = pl.BlockSpec(memory_space=pltpu.VMEM)
    dma = pltpu.SemaphoreType.DMA
    routing = (counts, weights, slide_of, owner_map)
    grad, den = pl.pallas_call(
        functools.partial(gather_kernel, sz),
        out_shape=(
            jax.ShapeDtypeStruct((SLOTS, pairs, LANES), f32),
            jax.ShapeDtypeStruct((pairs, LANES), f32),
        ),
        in_specs=[smem] * 4 + [vmem],
        out_specs=(vmem, vmem),
        scratch_shapes=[
            pltpu.VMEM((pairs, LANES), f32),
            pltpu.VMEM((sz.tiles, pairs, LANES), bf16),
            pltpu.VMEM((8, LANES), f32),
            pltpu.VMEM((sz.nz - 1, 8, LANES), f32),
            pltpu.VMEM((sz.nx - 1, 8, LANES), f32),
            pltpu.VMEM((8, LANES), f32),
        ]
        + [dma((sz.nz - 1,))] * 2
        + [dma((sz.nx - 1,))] * 2
        + [dma((sz.nz - 1,))] * 2
        + [dma((sz.nx - 1,))] * 2,
        compiler_params=pltpu.CompilerParams(collective_id=0, has_side_effects=True),
        name="gather",
    )(*routing, cot)

    input_grad, terms, parts = pl.pallas_call(
        functools.partial(compute_kernel, sz),
        grid=(pairs,),
        out_shape=(
            jax.ShapeDtypeStruct((1, SLOTS, SIDE, SIDE, channels), f32),
            jax.ShapeDtypeStruct((2, pairs, PACKED, LANES), bf16),
            jax.ShapeDtypeStruct((sz.tiles, pairs, LANES), f32),
        ),
        in_specs=[smem] * 4
        + [
            pl.BlockSpec((1, SLOTS, SIDE, SIDE, LANES), lambda p: (0, 0, 0, 0, p)),
            pl.BlockSpec((TAPS, WIDTH, LANES), lambda p: (0, 0, p)),
            vmem,
        ],
        out_specs=(
            pl.BlockSpec((1, SLOTS, SIDE, SIDE, LANES), lambda p: (0, 0, 0, 0, p)),
            pl.BlockSpec((2, 1, PACKED, LANES), lambda p: (0, p, 0, 0)),
            pl.BlockSpec((sz.tiles, pairs, LANES), lambda p: (0, 0, 0)),
        ),
        scratch_shapes=[
            pltpu.VMEM((PADDED, LANES), f32),
            pltpu.VMEM((PADDED, LANES), f32),
            pltpu.VMEM((ROWS, TAPS * LANES), bf16),
            pltpu.VMEM((ROWS, TAPS * LANES), bf16),
            pltpu.VMEM((TAPS * LANES, LANES), bf16),
            pltpu.VMEM((LANES, TAPS * LANES), bf16),
        ],
        compiler_params=pltpu.CompilerParams(
            dimension_semantics=("arbitrary",), vmem_limit_bytes=40 * 1024 * 1024
        ),
        name="compute",
    )(*routing, tiles, conv_weight, grad)

    piece_pad = (sz.piece + 15) // 16 * 16
    pooled, result = pl.pallas_call(
        functools.partial(reduce_kernel, sz),
        out_shape=(
            jax.ShapeDtypeStruct((pairs, LANES), f32),
            jax.ShapeDtypeStruct((PACKED, LANES), f32),
        ),
        in_specs=[vmem] * 3,
        out_specs=(vmem, vmem),
        scratch_shapes=[
            pltpu.VMEM((pairs, PACKED, LANES), bf16),
            pltpu.VMEM((pairs, PACKED, LANES), bf16),
            pltpu.VMEM((sz.ny - 1, sz.nx, PACKED, LANES), bf16),
            pltpu.VMEM((sz.nx, PACKED, LANES), bf16),
            pltpu.VMEM((sz.nx - 1, PACKED, LANES), bf16),
            pltpu.VMEM((PACKED, LANES), f32),
            pltpu.VMEM((sz.nz, piece_pad, LANES), bf16),
            pltpu.VMEM((sz.nz - 1, piece_pad, LANES), bf16),
            pltpu.VMEM((piece_pad, LANES), f32),
            pltpu.VMEM((sz.nz, piece_pad, LANES), f32),
            pltpu.VMEM((sz.nx - 1, sz.nz, pairs, LANES), f32),
            pltpu.VMEM((sz.nz, pairs, LANES), f32),
            pltpu.VMEM((sz.nz - 1, pairs, LANES), f32),
        ]
        + [dma((sz.ny,))] * 2
        + [dma((sz.ny - 1,))] * 2
        + [dma((sz.nx - 1,))] * 2
        + [dma((sz.nz - 1,))] * 2
        + [dma((sz.slides,)), dma((sz.nz,))]
        + [dma((sz.nx - 1,))] * 2
        + [dma((sz.nz - 1,))] * 2,
        compiler_params=pltpu.CompilerParams(
            collective_id=1, has_side_effects=True, vmem_limit_bytes=40 * 1024 * 1024
        ),
        name="reduce",
    )(terms, parts, den)
    weight_grad = result.reshape(TAPS, 32, 2, WIDTH).transpose(0, 3, 2, 1).reshape(TAPS, WIDTH, WIDTH)
    return pooled.reshape(1, 1, channels), input_grad, weight_grad


def solution(mesh):
    sz = Sizes(mesh)
    return jax.shard_map(
        functools.partial(shards, sz),
        mesh=mesh,
        in_specs=(
            P("slide", "tile", None, None, None),
            P("slide", "tile"),
            P("slide", "tile"),
            P("slide", "tile", None),
            P("slide", None),
            P("slide", "tile", None),
            P(),
        ),
        out_specs=(
            P("slide", "tile", None),
            P("slide", "tile", None, None, None),
            P(None, None, "tile"),
        ),
        check_vma=False,
    )
```

time: 554 us -> 101 us (0.18)
  the two profiles are of different devices: /device:TPU:1 before, /device:TPU:5 now
where the time goes in v1:
time: 101 us
  Pallas kernels  88.6 us (88%)
  local copies, waits for them, and re-layouts  10.8 us (11%)
  between operations  1.34 us (1%)
    pallas_call x1, Pallas kernels, shards(): pl.pallas_call(functools.partial(reduce_kernel, sz), out_shape=(jax.Shape...  58.3 us
    pallas_call x1, Pallas kernels, shards(): pl.pallas_call(functools.partial(compute_kernel, sz), grid=(pairs,), out_...  15.5 us
    pallas_call x1, Pallas kernels, shards(): pl.pallas_call(functools.partial(gather_kernel, sz), out_shape=(jax.Shape...  14.8 us
    unnamed x18, local copies, waits for them, and re-layouts  10.5 us

profile of v1, /device:TPU:5, one launch (start us, length us, event | category | flops | bytes accessed | tf_op | source)
XLA Modules:
  0.0 100.7 jit_solution(12450028343126025643)
XLA Ops:
  1.3 1.3 %copy.15.slide_of = s32[1,3,1]{2,1,0:T(4,128)} copy(s32[1,3,1]{1,2,0:T(1,128)} %param.10) | data formatting | bytes 24 | tf_op args[3]
  2.6 14.8 %gather.1 = (f32[3,16,128]{2,1,0:T(8,128)}, f32[16,128]{1,0:T(8,128)}) custom-call(s32[1,1]{1,0:T(1,128)S(6)} %copy.20.counts, f32[1,3]{1,0:T(1,128)} %weights.3, s32[1,3,1]{2,1,0:T(4,128)} %copy.15.slide_of, s32[1,32]{1,0:T(1,128)} %owner_map.3, bf16[1,1,2048]{2,1,0:T(2,128)(2,1)} %cot.1), custom_call_target="tpu_custom_call" | custom-call | tf_op jit(solution)/shard_map/gather/pallas_call | solution.py:322
  17.4 0.0 copy-start
  17.4 1.7 %copy-done = bf16[9,64,2048]{2,1,0:T(8,128)(2,1)S(1)} copy-done((bf16[9,64,2048]{2,1,0:T(8,128)(2,1)S(1)}, bf16[9,64,2048]{2,1,0:T(8,128)(2,1)}, u32[]{:S(2)}) %copy-start) | copy-done | bytes 2359320
  19.1 0.0 copy-start.1
  19.1 1.1 %copy-done.1 = bf16[1,3,7,7,2048]{4,3,2,1,0:T(8,128)(2,1)S(1)} copy-done((bf16[1,3,7,7,2048]{4,3,2,1,0:T(8,128)(2,1)S(1)}, bf16[1,3,7,7,2048]{4,3,2,1,0:T(8,128)(2,1)}, u32[]{:S(2)}) %copy-start.1) | copy-done | bytes 602136
  20.2 0.0 copy-start.2
  20.2 0.7 copy-done.2
  20.9 0.0 copy-start.3
  20.9 0.7 copy-done.3
  21.6 0.0 copy-start.5
  21.6 0.7 copy-done.5
  22.3 0.0 copy-start.6
  22.3 0.7 copy-done.6
  22.9 0.0 copy-start.4
  22.9 15.5 %compute.1 = (f32[1,3,7,7,2048]{4,3,2,1,0:T(8,128)S(1)}, bf16[2,16,288,128]{3,2,1,0:T(8,128)(2,1)S(1)}, f32[32,16,128]{2,1,0:T(8,128)S(1)}) custom-call(s32[1,1]{1,0:T(1,128)S(6)} %copy.20.counts, f32[1,3]{1,0:T(1,128)S(1)} %copy-done.5, s32[1,3,1]{2,1,0:T(4,128)S(1)} %copy-done.3, s32[1,32]{1,0:T(1,128)S(1)} %copy-done.6, ...), custom_call_target="tpu_custom_call" | custom-call | tf_op jit(solution)/shard_map/compute/pallas_call | solution.py:346
  38.4 0.0 copy-done.4
  38.4 58.3 %reduce.1 = (f32[16,128]{1,0:T(8,128)S(1)}, f32[288,128]{1,0:T(8,128)S(1)}) custom-call(bf16[2,16,288,128]{3,2,1,0:T(8,128)(2,1)S(1)} %get-tuple-element.11.terms, f32[32,16,128]{2,1,0:T(8,128)S(1)} %get-tuple-element.12.parts, f32[16,128]{1,0:T(8,128)S(1)} %copy-done.4), custom_call_target="tpu_custom_call" | custom-call | tf_op jit(solution)/shard_map/reduce/pallas_call | solution.py:380
  96.7 0.2 reshape.16
  97.0 0.9 copy.18
  97.9 2.3 %copy.17 = f32[1,3,7,7,2048]{4,0,3,2,1:T(1,128)} copy(f32[1,3,7,7,2048]{4,3,2,1,0:T(8,128)S(1)} %get-tuple-element.21) | data formatting | bytes 2408448
  100.1 0.6 copy.21
  (1 shorter events, 0.0 us)
Async XLA Ops:
  17.4 1.7 %copy-start = (bf16[9,64,2048]{2,1,0:T(8,128)(2,1)S(1)}, bf16[9,64,2048]{2,1,0:T(8,128)(2,1)}, u32[]{:S(2)}) copy-start(bf16[9,64,2048]{2,1,0:T(8,128)(2,1)} %weight.1) | copy-start | bytes 7077892
  19.1 1.1 %copy-start.1 = (bf16[1,3,7,7,2048]{4,3,2,1,0:T(8,128)(2,1)S(1)}, bf16[1,3,7,7,2048]{4,3,2,1,0:T(8,128)(2,1)}, u32[]{:S(2)}) copy-start(bf16[1,3,7,7,2048]{4,3,2,1,0:T(8,128)(2,1)} %tiles.1) | copy-start | bytes 1806340
  20.2 0.7 copy-start.2
  20.9 0.7 copy-start.3
  21.6 0.7 copy-start.5
  22.3 0.7 copy-start.6
  22.9 15.5 %copy-start.4 = (f32[16,128]{1,0:T(8,128)S(1)}, f32[16,128]{1,0:T(8,128)}, u32[]{:S(2)}) copy-start(f32[16,128]{1,0:T(8,128)} %get-tuple-element.13.den) | copy-start | bytes 24580

commit v2 on v0

v2 whole, which is shorter than its diff:
```python
import functools

import jax
import jax.numpy as jnp
from jax import lax
from jax.experimental import pallas as pl
from jax.experimental.pallas import tpu as pltpu
from jax.sharding import PartitionSpec as P

MESH = pl.DeviceIdType.MESH
LOSS_SCALE = 512.0
SIDE = 7
SLOTS = 3
WIDTH = 64
LANES = 128
TAPS = 9
ROWS = SLOTS * 64
BASE = 16
PADDED = BASE + ROWS + 16
f32 = jnp.float32
bf16 = jnp.bfloat16


class Sizes:
    def __init__(self, mesh):
        self.tiles = mesh.shape["tile"]
        self.slides = mesh.shape["slide"]
        self.ny = self.slides // 2
        self.nx = self.ny
        self.nz = self.tiles // self.nx
        self.pairs = self.tiles // 2
        self.share = 32 // self.ny
        self.packed = TAPS * self.share
        self.packed_pad = (self.packed + 15) // 16 * 16


def position(sz):
    tile = lax.axis_index("tile")
    slide = lax.axis_index("slide")
    return tile, slide, tile // sz.nz, tile % sz.nz, slide // 2, slide % 2


def remote(src, dst, send, recv, device):
    return pltpu.make_async_remote_copy(
        src_ref=src, dst_ref=dst, send_sem=send, recv_sem=recv, device_id=device, device_id_type=MESH
    )


def signal(device):
    pl.semaphore_signal(pltpu.get_barrier_semaphore(), inc=1, device_id=device, device_id_type=MESH)


def slot_route(slot, counts, weights, slide_of, owner_map):
    coef = jnp.where(slot < counts[0, 0], weights[0, slot], 0.0)
    return coef, owner_map[0, slide_of[0, slot]]


C_LAG = 2
Y_LAG = 5
BARRIER_STEP = 1
Z_STEP = 6
P_STEP = 5


def fused_kernel(
    sz, counts, weights, slide_of, owner_map, cot, tiles_hbm, weight_hbm,
    pooled, input_grad, result,
    tiles, weight, stage, all_cot, my_total, z_total, x_total, total, grad,
    xp, gp, xc, gc, w_rows, w_lanes, slopes, parts,
    terms, c_in, s1, y_in, s2, o_in, own, fin, px_in, psum, pz_in,
    tile_sem, weight_sem, gzs, gzr, gxs, gxr, tzs, tzr, txs, txr,
    cs, cr, ys, yr, os, orr, fs, fr, pxs, pxr, pzs, pzr,
):
    tile, slide, x, z, y, c = position(sz)
    nx, ny, nz, pairs = sz.nx, sz.ny, sz.nz, sz.pairs
    share, packed = sz.share, sz.packed
    z_peers = [(x * nz + (z + off) % nz, slide) for off in range(1, nz)]
    x_peers = [(((x + off) % nx) * nz + z, slide) for off in range(1, nx)]
    mate = (tile, y * 2 + 1 - c)
    y_peers = [(tile, ((y + off) % ny) * 2 + c) for off in range(1, ny)]
    is_owner = (z % 2) == c

    def pair_at(s):
        return (tile // 2 + 1 + s) % pairs

    def lanes_of(s):
        return pl.ds(pl.multiple_of(pair_at(s) * LANES, LANES), LANES)

    def load(s):
        lanes = lanes_of(s)
        return (
            pltpu.make_async_copy(tiles_hbm.at[0, :, :, :, lanes], tiles.at[s], tile_sem.at[s]),
            pltpu.make_async_copy(weight_hbm.at[:, :, lanes], weight.at[s], weight_sem.at[s]),
        )

    @pl.loop(0, pairs)
    def _(s):
        for copy in load(s):
            copy.start()

    @pl.loop(1, sz.tiles)
    def _(d):
        signal(((tile + d) % sz.tiles, slide))

    @pl.loop(1, sz.slides)
    def _(d):
        signal((tile, (slide + d) % sz.slides))

    xp[...] = jnp.zeros_like(xp)
    gp[...] = jnp.zeros_like(gp)
    for j in range(pairs):
        stage[pl.ds(j, 1), :] = cot[0, :, pl.ds(j * LANES, LANES)].astype(f32)
    all_cot[tile] = stage[...].astype(bf16)
    lane = lax.broadcasted_iota(jnp.int32, (8, LANES), 1)
    routes = [slot_route(s, counts, weights, slide_of, owner_map) for s in range(SLOTS)]
    mine = jnp.zeros((8, LANES), f32)
    for coef, target in routes:
        mine = mine + jnp.where(lane == target, coef, 0.0)
    my_total[...] = mine

    def total_z(i):
        return remote(my_total, z_total.at[i], tzs.at[i], tzr.at[i], z_peers[i])

    def rows_z(i, source):
        return remote(all_cot.at[source], all_cot.at[source], gzs.at[i], gzr.at[i], z_peers[i])

    def total_x(i):
        return remote(total, x_total.at[i], txs.at[i], txr.at[i], x_peers[i])

    def rows_x(i, source):
        block = all_cot.at[pl.ds(source * nz, nz)]
        return remote(block, block, gxs.at[i], gxr.at[i], x_peers[i])

    low64 = lax.broadcasted_iota(jnp.int32, (WIDTH, LANES), 1) < WIDTH
    row = lax.broadcasted_iota(jnp.int32, (64, LANES), 0)
    real = (row % 8 < SIDE) & (row < 8 * SIDE)
    owner_row = lax.broadcasted_iota(jnp.int32, (sz.tiles, LANES), 0)

    @pl.loop(0, pairs)
    def _(s):
        @pl.when(s == BARRIER_STEP)
        def _():
            pl.semaphore_wait(pltpu.get_barrier_semaphore(), sz.tiles + sz.slides - 2)
            for i in range(nz - 1):
                total_z(i).start()
                rows_z(i, tile).start()

        @pl.when(s == min(Z_STEP, pairs - 1))
        def _():
            v = my_total[...]
            for i in range(nz - 1):
                total_z(i).wait_recv()
                rows_z(i, x * nz + (z + nz - 1 - i) % nz).wait_recv()
                v = v + z_total[i]
            total[...] = v
            for i in range(nx - 1):
                total_x(i).start()
                rows_x(i, x).start()

        for copy in load(s):
            copy.wait()
        for tap in range(TAPS):
            w = weight[s, tap]
            zero = jnp.zeros_like(w)
            first, second = jnp.where(low64, w, zero), jnp.where(low64, zero, w)
            w_rows[pl.ds(tap * LANES, WIDTH), :] = first
            w_rows[pl.ds(tap * LANES + WIDTH, WIDTH), :] = second
            w_lanes[s, pl.ds(0, WIDTH), pl.ds(tap * LANES, LANES)] = first
            w_lanes[s, pl.ds(WIDTH, WIDTH), pl.ds(tap * LANES, LANES)] = second
        for t in range(SLOTS):
            for h in range(SIDE):
                xp[pl.ds(BASE + 64 * t + 8 * h, SIDE), :] = tiles[s, t, h].astype(f32)
        for tap in range(TAPS):
            shift = 8 * (tap // 3 - 1) + tap % 3 - 1
            xc[s, :, pl.ds(tap * LANES, LANES)] = xp[pl.ds(BASE + shift, ROWS), :].astype(bf16)
        pre = jnp.dot(xc[s], w_rows[...], preferred_element_type=f32)
        sigma = 1.0 / (1.0 + jnp.exp(-pre))
        part = jnp.zeros((sz.tiles, LANES), f32)
        for t in range(SLOTS):
            v, q = pre[64 * t : 64 * t + 64], sigma[64 * t : 64 * t + 64]
            mean = jnp.sum(jnp.where(real, v * q, 0.0), axis=0, keepdims=True) / (SIDE * SIDE)
            embedding = mean.astype(bf16).astype(f32)
            coef, target = routes[t]
            part = part + jnp.where(owner_row == target, coef, 0.0) * embedding
            slope = q * (1.0 + v * (1.0 - q))
            slopes[s, pl.ds(64 * t, 64), :] = jnp.where(real, slope, 0.0)
        parts[:, pl.ds(pair_at(s), 1), :] = part.reshape(sz.tiles, 1, LANES)

    def parts_x(i):
        xo = (x + i + 1) % nx
        return remote(parts.at[pl.ds(xo * nz, nz)], px_in.at[i], pxs.at[i], pxr.at[i], x_peers[i])

    def parts_z(i):
        return remote(psum.at[(z + i + 1) % nz], pz_in.at[i], pzs.at[i], pzr.at[i], z_peers[i])

    for i in range(nx - 1):
        parts_x(i).start()
    v = total[...]
    for i in range(nx - 1):
        total_x(i).wait_recv()
        rows_x(i, (x + nx - 1 - i) % nx).wait_recv()
        v = v + x_total[i]
    denominator = jnp.maximum(v, 1.0)

    def pick(owner):
        found = jnp.sum(jnp.where(lane == owner, denominator, 0.0), axis=1, keepdims=True)
        return jnp.broadcast_to(found[0:1], (pairs, LANES))

    for t, (coef, target) in enumerate(routes):
        scaled = (LOSS_SCALE * all_cot[target].astype(f32) / pick(target)).astype(bf16)
        grad[t] = coef * scaled.astype(f32)

    def swap(s):
        return remote(terms.at[1 - c, s], c_in.at[s], cs.at[s], cr.at[s], mate)

    def along_y(i, s):
        return remote(s1.at[s, (y + i + 1) % ny], y_in.at[i, s], ys.at[i, s], yr.at[i, s], y_peers[i])

    def to_owner(s):
        return remote(s2.at[s], o_in.at[tile], os.at[s], orr.at[tile], (2 * pair_at(s) + c, slide))

    low = lax.broadcasted_iota(jnp.int32, (32, LANES), 1) < WIDTH
    none = jnp.zeros((share, LANES), f32)

    @pl.loop(0, pairs + Y_LAG)
    def _(s):
        @pl.when(s < pairs)
        def _():
            for t in range(SLOTS):
                upstream = grad[t, pl.ds(pair_at(s), 1), :] / (SIDE * SIDE)
                gp[pl.ds(BASE + 64 * t, 64), :] = upstream * slopes[s, pl.ds(64 * t, 64), :]
            g = gp[pl.ds(BASE, ROWS), :].astype(bf16)
            dw = jnp.dot(g.T, xc[s], preferred_element_type=f32)
            even, odd = [], []
            for tap in range(TAPS):
                d = dw[:, tap * LANES : (tap + 1) * LANES]
                even.append(jnp.where(low, d[0:32], pltpu.roll(d[32:64], WIDTH, 1)))
                odd.append(jnp.where(low, pltpu.roll(d[64:96], WIDTH, 1), d[96:128]))
            per = 16 // share
            for parity, rows in enumerate((even, odd)):
                for yy in range(ny):
                    for j in range(sz.packed_pad // 16):
                        block = [
                            rows[tap][yy * share : (yy + 1) * share] if tap < TAPS else none
                            for tap in range(j * per, (j + 1) * per)
                        ]
                        terms[parity, s, yy, pl.ds(16 * j, 16), :] = jnp.concatenate(block, axis=0).astype(bf16)
            swap(s).start()
            for tap in range(TAPS):
                shift = 8 * (tap // 3 - 1) + tap % 3 - 1
                gc[:, pl.ds(tap * LANES, LANES)] = gp[pl.ds(BASE - shift, ROWS), :].astype(bf16)
            dx = lax.dot_general(
                gc[...], w_lanes[s], (((1,), (1,)), ((), ())), preferred_element_type=f32
            )
            lanes = lanes_of(s)
            for t in range(SLOTS):
                for h in range(SIDE):
                    at = 64 * t + 8 * h
                    input_grad[0, t, h, :, lanes] = dx[at : at + SIDE]

        @pl.when((s >= C_LAG) & (s < pairs + C_LAG))
        def _():
            r = s - C_LAG
            swap(r).wait_recv()
            s1[r] = (terms[c, r].astype(f32) + c_in[r].astype(f32)).astype(bf16)
            for i in range(ny - 1):
                along_y(i, r).start()

        @pl.when(s >= Y_LAG)
        def _():
            r = s - Y_LAG
            v = s1[r, y].astype(f32)
            for i in range(ny - 1):
                along_y(i, r).wait_recv()
                v = v + y_in[i, r].astype(f32)
            s2[r] = v.astype(bf16)

            @pl.when(2 * pair_at(r) + c != tile)
            def _():
                to_owner(r).start()

        @pl.when(s == P_STEP)
        def _():
            for i in range(nx - 1):
                parts_x(i).wait_recv()

            @pl.loop(0, nz)
            def _(k):
                v = parts[x * nz + k]
                for i in range(nx - 1):
                    v = v + px_in[i, k]
                psum[k] = v

            for i in range(nz - 1):
                parts_z(i).start()

    v = psum[z]
    for i in range(nz - 1):
        parts_z(i).wait_recv()
        v = v + pz_in[i]
    pooled[...] = v / pick(tile)

    finals = [(tile, (slide + d) % sz.slides) for d in range(1, sz.slides)]

    @pl.when(is_owner)
    def _():
        own[...] = s2[pairs - 1].astype(f32)

        @pl.loop(1, sz.tiles)
        def _(d):
            source = ((tile // 2) * 2 + sz.tiles - d) % sz.tiles
            source = source + (d // (sz.tiles - 1)) * ((tile // 2) * 2 + 1 - z % 2 - source)
            remote(s2.at[0], o_in.at[source], os.at[0], orr.at[source], mate).wait_recv()
            own[...] += o_in[source].astype(f32)

        own[...] = own[...] / LOSS_SCALE
        for d, peer in enumerate(finals):
            remote(own, fin.at[y], fs.at[d], fr.at[y], peer).start()
        fin[y] = own[...]

    for q in range(ny):

        @pl.when(jnp.logical_not(is_owner & (y == q)))
        def _():
            remote(own, fin.at[q], fs.at[0], fr.at[q], finals[0]).wait_recv()

    for tap in range(TAPS):
        rows = [fin[q, pl.ds(tap * share, share), :] for q in range(ny)]
        block = jnp.concatenate(rows, axis=0).T
        result[tap] = jnp.concatenate([block[0:WIDTH], block[WIDTH:]], axis=1)

    @pl.when(is_owner)
    def _():
        for d, peer in enumerate(finals):
            remote(own, fin.at[y], fs.at[d], fr.at[y], peer).wait_send()

    for i in range(nz - 1):
        total_z(i).wait_send()
        rows_z(i, tile).wait_send()
        parts_z(i).wait_send()
    for i in range(nx - 1):
        total_x(i).wait_send()
        rows_x(i, x).wait_send()
        parts_x(i).wait_send()

    @pl.loop(0, pairs)
    def _(s):
        swap(s).wait_send()
        for i in range(ny - 1):
            along_y(i, s).wait_send()

        @pl.when(2 * pair_at(s) + c != tile)
        def _():
            to_owner(s).wait_send()


def shards(sz, tiles, counts, weights, slide_of, owner_map, cot, conv_weight):
    pairs, channels = sz.pairs, sz.tiles * WIDTH
    smem = pl.BlockSpec(memory_space=pltpu.SMEM)
    vmem = pl.BlockSpec(memory_space=pltpu.VMEM)
    hbm = pl.BlockSpec(memory_space=pltpu.MemorySpace.HBM)
    dma = pltpu.SemaphoreType.DMA
    pad = sz.packed_pad
    pooled, input_grad, weight_grad = pl.pallas_call(
        functools.partial(fused_kernel, sz),
        out_shape=(
            jax.ShapeDtypeStruct((pairs, LANES), f32),
            jax.ShapeDtypeStruct((1, SLOTS, SIDE, SIDE, channels), f32),
            jax.ShapeDtypeStruct((TAPS, WIDTH, WIDTH), f32),
        ),
        in_specs=[smem] * 4 + [vmem] + [hbm] * 2,
        out_specs=(vmem, vmem, vmem),
        scratch_shapes=[
            pltpu.VMEM((pairs, SLOTS, SIDE, SIDE, LANES), bf16),
            pltpu.VMEM((pairs, TAPS, WIDTH, LANES), bf16),
            pltpu.VMEM((pairs, LANES), f32),
            pltpu.VMEM((sz.tiles, pairs, LANES), bf16),
            pltpu.VMEM((8, LANES), f32),
            pltpu.VMEM((sz.nz - 1, 8, LANES), f32),
            pltpu.VMEM((sz.nx - 1, 8, LANES), f32),
            pltpu.VMEM((8, LANES), f32),
            pltpu.VMEM((SLOTS, pairs, LANES), f32),
            pltpu.VMEM((PADDED, LANES), f32),
            pltpu.VMEM((PADDED, LANES), f32),
            pltpu.VMEM((pairs, ROWS, TAPS * LANES), bf16),
            pltpu.VMEM((ROWS, TAPS * LANES), bf16),
            pltpu.VMEM((TAPS * LANES, LANES), bf16),
            pltpu.VMEM((pairs, LANES, TAPS * LANES), bf16),
            pltpu.VMEM((pairs, ROWS, LANES), f32),
            pltpu.VMEM((sz.tiles, pairs, LANES), f32),
            pltpu.VMEM((2, pairs, sz.ny, pad, LANES), bf16),
            pltpu.VMEM((pairs, sz.ny, pad, LANES), bf16),
            pltpu.VMEM((pairs, sz.ny, pad, LANES), bf16),
            pltpu.VMEM((sz.ny - 1, pairs, pad, LANES), bf16),
            pltpu.VMEM((pairs, pad, LANES), bf16),
            pltpu.VMEM((sz.tiles, pad, LANES), bf16),
            pltpu.VMEM((pad, LANES), f32),
            pltpu.VMEM((sz.ny, pad, LANES), f32),
            pltpu.VMEM((sz.nx - 1, sz.nz, pairs, LANES), f32),
            pltpu.VMEM((sz.nz, pairs, LANES), f32),
            pltpu.VMEM((sz.nz - 1, pairs, LANES), f32),
        ]
        + [dma((pairs,))] * 2
        + [dma((sz.nz - 1,))] * 2
        + [dma((sz.nx - 1,))] * 2
        + [dma((sz.nz - 1,))] * 2
        + [dma((sz.nx - 1,))] * 2
        + [dma((pairs,))] * 2
        + [dma((sz.ny - 1, pairs))] * 2
        + [dma((pairs,)), dma((sz.tiles,))]
        + [dma((sz.slides,)), dma((sz.ny,))]
        + [dma((sz.nx - 1,))] * 2
        + [dma((sz.nz - 1,))] * 2,
        compiler_params=pltpu.CompilerParams(
            collective_id=0, has_side_effects=True, vmem_limit_bytes=56 * 1024 * 1024
        ),
        name="fused",
    )(counts, weights, slide_of[:, :, 0], owner_map, cot, tiles, conv_weight)
    return pooled.reshape(1, 1, channels), input_grad, weight_grad


def solution(mesh):
    sz = Sizes(mesh)
    return jax.shard_map(
        functools.partial(shards, sz),
        mesh=mesh,
        in_specs=(
            P("slide", "tile", None, None, None),
            P("slide", "tile"),
            P("slide", "tile"),
            P("slide", "tile", None),
            P("slide", None),
            P("slide", "tile", None),
            P(),
        ),
        out_specs=(
            P("slide", "tile", None),
            P("slide", "tile", None, None, None),
            P(None, None, "tile"),
        ),
        check_vma=False,
    )
```

time: 554 us -> 65.1 us (0.12); the launches traced: 546 us -> 64.9 us
  waiting for transfers between devices: 253 us -> 0 us
  blocking collectives: 111 us -> 0 us
  local copies, waits for them, and re-layouts: 99.6 us -> 4.97 us
  matrix products: 61 us -> 0 us
  Pallas kernels: 0 us -> 58.7 us
  between operations: 16 us -> 1.3 us
    unnamed x3 -> x0, waiting for transfers between devices: 192 us -> none
    all_gather x3 -> x0, blocking collectives: 111 us -> none  [the longest x1 40.3 us: shards(): shares = lax.all_gather(routing, 'tile', axis=1, tiled=True)]
    dot_general x29 -> x0, matrix products: 61 us -> none  [the longest x9 22.9 us: conv_backward(): jnp.einsum('nhwgi,nhwgo->igo', window, grads_split, preferred_element_typ...]
    psum x1 -> x0, waiting for transfers between devices: 60.9 us -> none  [shards(): reduced = lax.psum(shard_sum, 'slide')]
    pallas_call x0 -> x1, Pallas kernels: none -> 58.7 us  [shards(): pl.pallas_call(functools.partial(fused_kernel, sz), out_shape=(jax.ShapeD...]
    another operation x20 -> x0, local copies, waits for them, and re-layouts: 32.9 us -> none  [the longest x10 19.1 us: conv_backward(): return (input_grads, jnp.stack(pieces, axis=0))]
    unnamed x79 -> x7, local copies, waits for them, and re-layouts: 37.2 us -> 4.97 us
    reshape x9 -> x0, local copies, waits for them, and re-layouts: 22.6 us -> none  [conv_forward(): padded[:, row_off:row_off + spatial, col_off:col_off + spatial, :]]
  transfers between devices with their start and end apart: 2 -> 0, of which waited for: 2 -> 0; matrix products, arithmetic and copies ran while one was open for 4% -> 0% of each run, Pallas kernels for 0% -> 0%
where the time goes in v2:
time: 65.1 us; the launch traced here: 64.9 us
  Pallas kernels  58.7 us (90%)
  local copies, waits for them, and re-layouts  4.97 us (8%)
  between operations  1.3 us (2%)
    pallas_call x1, Pallas kernels, shards(): pl.pallas_call(functools.partial(fused_kernel, sz), out_shape=(jax.ShapeD...  58.7 us
    unnamed x7, local copies, waits for them, and re-layouts  4.97 us

profile of v2, /device:TPU:1, one launch (start us, length us, event | category | flops | bytes accessed | tf_op | source)
XLA Modules:
  0.0 64.9 jit_solution(4156768965776239190)
XLA Ops:
  1.3 58.7 %fused.1 = (f32[16,128]{1,0:T(8,128)}, f32[1,3,7,7,2048]{4,3,2,1,0:T(8,128)}, f32[9,64,64]{2,1,0:T(8,128)}) custom-call(s32[1,1]{1,0:T(1,128)S(6)} %copy.13.counts, f32[1,3]{1,0:T(1,128)} %weights.1, s32[1,3]{1,0:T(1,128)} %bitcast.3, s32[1,32]{1,0:T(1,128)} %owner_map.1, bf16[1,1,2048]{2,1,0:T(2,128)(2,1)} %cot.1, bf16[1,3,7,7,2048]{4,3,2,1,0:T(8,128)(2,1)} %tiles_hbm.1, ...), custom_call_target="tpu_custom_call" | custom-call | tf_op jit(solution)/shard_map/fused/pallas_call | solution.py:364
  60.0 0.0 copy-start.1
  60.0 0.0 copy-start
  60.0 3.6 %copy.10 = f32[1,3,7,7,2048]{4,0,3,2,1:T(1,128)} copy(f32[1,3,7,7,2048]{4,3,2,1,0:T(8,128)} %get-tuple-element.10) | data formatting | bytes 2408448
  63.6 0.0 copy-done.1
  63.6 0.6 copy.14
  64.2 0.0 copy-done
  64.2 0.7 %copy.15 = f32[9,64,64]{2,1,0:T(8,128)} copy(f32[9,64,64]{2,1,0:T(8,128)S(1)} %copy-done) | data formatting | bytes 294912
Async XLA Ops:
  60.0 3.7 %copy-start.1 = (f32[16,128]{1,0:T(8,128)S(1)}, f32[16,128]{1,0:T(8,128)}, u32[]{:S(2)}) copy-start(f32[16,128]{1,0:T(8,128)} %get-tuple-element.6) | copy-start | bytes 24580
  60.0 4.3 %copy-start = (f32[9,64,64]{2,1,0:T(8,128)S(1)}, f32[9,64,64]{2,1,0:T(8,128)}, u32[]{:S(2)}) copy-start(f32[9,64,64]{2,1,0:T(8,128)} %get-tuple-element.17) | copy-start | bytes 442372

commit v3 on v2

--- a/solution.py
+++ b/solution.py
@@ -55,8 +55,9 @@
     return coef, owner_map[0, slide_of[0, slot]]
 
 
-C_LAG = 2
-Y_LAG = 5
+C_LAG = 4
+Y_LAG = 9
+X_LAG = 9
 BARRIER_STEP = 1
 Z_STEP = 6
 P_STEP = 5
@@ -67,7 +68,7 @@
     pooled, input_grad, result,
     tiles, weight, stage, all_cot, my_total, z_total, x_total, total, grad,
     xp, gp, xc, gc, w_rows, w_lanes, slopes, parts,
-    terms, c_in, s1, y_in, s2, o_in, own, fin, px_in, psum, pz_in,
+    terms, c_in, s1, y_in, s2, o_in, own, final, fin, px_in, psum, pz_in,
     tile_sem, weight_sem, gzs, gzr, gxs, gxr, tzs, tzr, txs, txr,
     cs, cr, ys, yr, os, orr, fs, fr, pxs, pxr, pzs, pzr,
 ):
@@ -222,14 +223,15 @@
     low = lax.broadcasted_iota(jnp.int32, (32, LANES), 1) < WIDTH
     none = jnp.zeros((share, LANES), f32)
 
+    def pre_grad(s):
+        upstream = [grad[t, pl.ds(pair_at(s), 1), :] / (SIDE * SIDE) for t in range(SLOTS)]
+        return [upstream[t] * slopes[s, pl.ds(64 * t, 64), :] for t in range(SLOTS)]
+
     @pl.loop(0, pairs + Y_LAG)
     def _(s):
         @pl.when(s < pairs)
         def _():
-            for t in range(SLOTS):
-                upstream = grad[t, pl.ds(pair_at(s), 1), :] / (SIDE * SIDE)
-                gp[pl.ds(BASE + 64 * t, 64), :] = upstream * slopes[s, pl.ds(64 * t, 64), :]
-            g = gp[pl.ds(BASE, ROWS), :].astype(bf16)
+            g = jnp.concatenate(pre_grad(s), axis=0).astype(bf16)
             dw = jnp.dot(g.T, xc[s], preferred_element_type=f32)
             even, odd = [], []
             for tap in range(TAPS):
@@ -246,17 +248,23 @@
                         ]
                         terms[parity, s, yy, pl.ds(16 * j, 16), :] = jnp.concatenate(block, axis=0).astype(bf16)
             swap(s).start()
+
+        @pl.when((s >= X_LAG) & (s < pairs + X_LAG))
+        def _():
+            r = s - X_LAG
+            for t, rows in enumerate(pre_grad(r)):
+                gp[pl.ds(BASE + 64 * t, 64), :] = rows
             for tap in range(TAPS):
                 shift = 8 * (tap // 3 - 1) + tap % 3 - 1
                 gc[:, pl.ds(tap * LANES, LANES)] = gp[pl.ds(BASE - shift, ROWS), :].astype(bf16)
             dx = lax.dot_general(
-                gc[...], w_lanes[s], (((1,), (1,)), ((), ())), preferred_element_type=f32
+                gc[...], w_lanes[r], (((1,), (1,)), ((), ())), preferred_element_type=f32
             )
-            lanes = lanes_of(s)
+            lanes = lanes_of(r)
             for t in range(SLOTS):
                 for h in range(SIDE):
                     at = 64 * t + 8 * h
-                    input_grad[0, t, h, :, lanes] = dx[at : at + SIDE]
+                    input_grad[t, h, :, :, lanes] = dx[at : at + SIDE].reshape(SIDE, 1, LANES)
 
         @pl.when((s >= C_LAG) & (s < pairs + C_LAG))
         def _():
@@ -313,26 +321,27 @@
             remote(s2.at[0], o_in.at[source], os.at[0], orr.at[source], mate).wait_recv()
             own[...] += o_in[source].astype(f32)
 
-        own[...] = own[...] / LOSS_SCALE
+        final[...] = (own[...] / LOSS_SCALE).astype(bf16)
         for d, peer in enumerate(finals):
-            remote(own, fin.at[y], fs.at[d], fr.at[y], peer).start()
-        fin[y] = own[...]
+            remote(final, fin.at[y], fs.at[d], fr.at[y], peer).start()
+        fin[y] = final[...]
 
     for q in range(ny):
 
         @pl.when(jnp.logical_not(is_owner & (y == q)))
         def _():
-            remote(own, fin.at[q], fs.at[0], fr.at[q], finals[0]).wait_recv()
-
+            remote(final, fin.at[q], fs.at[0], fr.at[q], finals[0]).wait_recv()
+
+    every = [fin[q].astype(f32) for q in range(ny)]
     for tap in range(TAPS):
-        rows = [fin[q, pl.ds(tap * share, share), :] for q in range(ny)]
+        rows = [v[tap * share : (tap + 1) * share] for v in every]
         block = jnp.concatenate(rows, axis=0).T
         result[tap] = jnp.concatenate([block[0:WIDTH], block[WIDTH:]], axis=1)
 
     @pl.when(is_owner)
     def _():
         for d, peer in enumerate(finals):
-            remote(own, fin.at[y], fs.at[d], fr.at[y], peer).wait_send()
+            remote(final, fin.at[y], fs.at[d], fr.at[y], peer).wait_send()
 
     for i in range(nz - 1):
         total_z(i).wait_send()
@@ -365,7 +374,7 @@
         functools.partial(fused_kernel, sz),
         out_shape=(
             jax.ShapeDtypeStruct((pairs, LANES), f32),
-            jax.ShapeDtypeStruct((1, SLOTS, SIDE, SIDE, channels), f32),
+            jax.ShapeDtypeStruct((SLOTS, SIDE, SIDE, 1, channels), f32),
             jax.ShapeDtypeStruct((TAPS, WIDTH, WIDTH), f32),
         ),
         in_specs=[smem] * 4 + [vmem] + [hbm] * 2,
@@ -395,7 +404,8 @@
             pltpu.VMEM((pairs, pad, LANES), bf16),
             pltpu.VMEM((sz.tiles, pad, LANES), bf16),
             pltpu.VMEM((pad, LANES), f32),
-            pltpu.VMEM((sz.ny, pad, LANES), f32),
+            pltpu.VMEM((pad, LANES), bf16),
+            pltpu.VMEM((sz.ny, pad, LANES), bf16),
             pltpu.VMEM((sz.nx - 1, sz.nz, pairs, LANES), f32),
             pltpu.VMEM((sz.nz, pairs, LANES), f32),
             pltpu.VMEM((sz.nz - 1, pairs, LANES), f32),
@@ -416,6 +426,7 @@
         ),
         name="fused",
     )(counts, weights, slide_of[:, :, 0], owner_map, cot, tiles, conv_weight)
+    input_grad = input_grad.reshape(1, SLOTS, SIDE, SIDE, channels)
     return pooled.reshape(1, 1, channels), input_grad, weight_grad
 
 

time: 65.1 us -> 59.9 us (0.920)
  Pallas kernels: 58.7 us -> 53.2 us
    pallas_call x1, Pallas kernels: 58.7 us -> 53.2 us  [shards(): pl.pallas_call(functools.partial(fused_kernel, sz), out_shape=(jax.ShapeD...]
    unnamed x7 -> x5, local copies, waits for them, and re-layouts: 4.97 us -> 5.18 us
where the time goes in v3:
time: 59.9 us; the launch traced here: 59.7 us
  Pallas kernels  53.2 us (89%)
  local copies, waits for them, and re-layouts  5.18 us (9%)
  between operations  1.29 us (2%)
    pallas_call x1, Pallas kernels, shards(): pl.pallas_call(functools.partial(fused_kernel, sz), out_shape=(jax.ShapeD...  53.2 us
    unnamed x5, local copies, waits for them, and re-layouts  5.18 us

profile of v3, /device:TPU:1, one launch (start us, length us, event | category | flops | bytes accessed | tf_op | source)
XLA Modules:
  0.0 59.7 jit_solution(13448066240640814529)
XLA Ops:
  1.3 53.2 %fused.1 = (f32[16,128]{1,0:T(8,128)}, f32[3,7,7,1,2048]{4,3,2,1,0:T(1,128)}, f32[9,64,64]{2,1,0:T(8,128)}) custom-call(s32[1,1]{1,0:T(1,128)S(6)} %copy.13.counts, f32[1,3]{1,0:T(1,128)} %weights.1, s32[1,3]{1,0:T(1,128)} %bitcast.5, s32[1,32]{1,0:T(1,128)} %owner_map.1, bf16[1,1,2048]{2,1,0:T(2,128)(2,1)} %cot.1, bf16[1,3,7,7,2048]{4,3,2,1,0:T(8,128)(2,1)} %tiles_hbm.1, ...), custom_call_target="tpu_custom_call" | custom-call | tf_op jit(solution)/shard_map/fused/pallas_call | solution.py:373
  54.5 1.3 %copy.14 = f32[1,1,2048]{2,1,0:T(1,128)} copy(f32[1,1,2048]{2,1,0:T(1,128)} %bitcast.4) | data formatting | bytes 16384
  55.8 0.0 copy-start
  55.8 3.2 %copy.15 = f32[1,3,7,7,2048]{4,0,3,2,1:T(1,128)} copy(f32[1,3,7,7,2048]{4,0,3,2,1:T(1,128)} %bitcast.3) | data formatting | bytes 2408448
  58.9 0.0 copy-done
  59.0 0.7 %copy.16 = f32[9,64,64]{2,1,0:T(8,128)} copy(f32[9,64,64]{2,1,0:T(8,128)S(1)} %copy-done) | data formatting | bytes 294912
Async XLA Ops:
  55.8 3.2 %copy-start = (f32[9,64,64]{2,1,0:T(8,128)S(1)}, f32[9,64,64]{2,1,0:T(8,128)}, u32[]{:S(2)}) copy-start(f32[9,64,64]{2,1,0:T(8,128)} %get-tuple-element.14) | copy-start | bytes 442372

commit v4 on v3

--- a/solution.py
+++ b/solution.py
@@ -67,22 +67,25 @@
     sz, counts, weights, slide_of, owner_map, cot, tiles_hbm, weight_hbm,
     pooled, input_grad, result,
     tiles, weight, stage, all_cot, my_total, z_total, x_total, total, grad,
-    xp, gp, xc, gc, w_rows, w_lanes, slopes, parts,
-    terms, c_in, s1, y_in, s2, o_in, own, final, fin, px_in, psum, pz_in,
+    xp, gp, xc, gc, w_rows, w_lanes, slopes, parts, parts16,
+    terms, c_in, s1, y_in, s2, x_in, s3, o_in, own, final, fin, px_in, psum, pz_in,
     tile_sem, weight_sem, gzs, gzr, gxs, gxr, tzs, tzr, txs, txr,
-    cs, cr, ys, yr, os, orr, fs, fr, pxs, pxr, pzs, pzr,
+    cs, cr, ys, yr, os, orr, xs, xr, os3, fs, fr, pxs, pxr, pzs, pzr,
 ):
     tile, slide, x, z, y, c = position(sz)
     nx, ny, nz, pairs = sz.nx, sz.ny, sz.nz, sz.pairs
-    share, packed = sz.share, sz.packed
+    share, nk = sz.share, nz // 2
     z_peers = [(x * nz + (z + off) % nz, slide) for off in range(1, nz)]
     x_peers = [(((x + off) % nx) * nz + z, slide) for off in range(1, nx)]
     mate = (tile, y * 2 + 1 - c)
     y_peers = [(tile, ((y + off) % ny) * 2 + c) for off in range(1, ny)]
     is_owner = (z % 2) == c
 
+    def owner_k(s):
+        return (z // 2 + 1 + s // nx) % nk
+
     def pair_at(s):
-        return (tile // 2 + 1 + s) % pairs
+        return ((x + 1 + s % nx) % nx) * nk + owner_k(s)
 
     def lanes_of(s):
         return pl.ds(pl.multiple_of(pair_at(s) * LANES, LANES), LANES)
@@ -99,13 +102,9 @@
         for copy in load(s):
             copy.start()
 
-    @pl.loop(1, sz.tiles)
-    def _(d):
-        signal(((tile + d) % sz.tiles, slide))
-
-    @pl.loop(1, sz.slides)
-    def _(d):
-        signal((tile, (slide + d) % sz.slides))
+    partners = z_peers + x_peers + y_peers + [mate]
+    for peer in partners:
+        signal(peer)
 
     xp[...] = jnp.zeros_like(xp)
     gp[...] = jnp.zeros_like(gp)
@@ -141,7 +140,7 @@
     def _(s):
         @pl.when(s == BARRIER_STEP)
         def _():
-            pl.semaphore_wait(pltpu.get_barrier_semaphore(), sz.tiles + sz.slides - 2)
+            pl.semaphore_wait(pltpu.get_barrier_semaphore(), len(partners))
             for i in range(nz - 1):
                 total_z(i).start()
                 rows_z(i, tile).start()
@@ -189,11 +188,12 @@
 
     def parts_x(i):
         xo = (x + i + 1) % nx
-        return remote(parts.at[pl.ds(xo * nz, nz)], px_in.at[i], pxs.at[i], pxr.at[i], x_peers[i])
+        return remote(parts16.at[pl.ds(xo * nz, nz)], px_in.at[i], pxs.at[i], pxr.at[i], x_peers[i])
 
     def parts_z(i):
         return remote(psum.at[(z + i + 1) % nz], pz_in.at[i], pzs.at[i], pzr.at[i], z_peers[i])
 
+    parts16[...] = parts[...].astype(bf16)
     for i in range(nx - 1):
         parts_x(i).start()
     v = total[...]
@@ -218,7 +218,24 @@
         return remote(s1.at[s, (y + i + 1) % ny], y_in.at[i, s], ys.at[i, s], yr.at[i, s], y_peers[i])
 
     def to_owner(s):
-        return remote(s2.at[s], o_in.at[tile], os.at[s], orr.at[tile], (2 * pair_at(s) + c, slide))
+        device = (2 * pair_at(s) + c, slide)
+        return remote(s2.at[s], o_in.at[z, x], os.at[s], orr.at[z, x], device)
+
+    def along_x(s):
+        device = (((x + 1 + s % nx) % nx) * nz + z, slide)
+        m, i = s // (2 * nx), s % nx
+        return remote(s1.at[s], x_in.at[m, i], xs.at[m, i], xr.at[m, i], device)
+
+    def to_owner_y(s, q):
+        device = (x * nz + 2 * owner_k(s) + c, q * 2 + c)
+        m = s // (2 * nx)
+        return remote(s3.at[m, q], o_in.at[z, y], os3.at[m, q], orr.at[z, y], device)
+
+    def by_y(s):
+        return (s // nx) % 2 == 0
+
+    def mine_at(s, q):
+        return is_owner & (owner_k(s) == z // 2) & (q == y)
 
     low = lax.broadcasted_iota(jnp.int32, (32, LANES), 1) < WIDTH
     none = jnp.zeros((share, LANES), f32)
@@ -271,10 +288,17 @@
             r = s - C_LAG
             swap(r).wait_recv()
             s1[r] = (terms[c, r].astype(f32) + c_in[r].astype(f32)).astype(bf16)
-            for i in range(ny - 1):
-                along_y(i, r).start()
-
-        @pl.when(s >= Y_LAG)
+
+            @pl.when(by_y(r))
+            def _():
+                for i in range(ny - 1):
+                    along_y(i, r).start()
+
+            @pl.when(jnp.logical_not(by_y(r)) & (r % nx != nx - 1))
+            def _():
+                along_x(r).start()
+
+        @pl.when((s >= Y_LAG) & by_y(s - Y_LAG))
         def _():
             r = s - Y_LAG
             v = s1[r, y].astype(f32)
@@ -282,10 +306,22 @@
                 along_y(i, r).wait_recv()
                 v = v + y_in[i, r].astype(f32)
             s2[r] = v.astype(bf16)
-
-            @pl.when(2 * pair_at(r) + c != tile)
-            def _():
-                to_owner(r).start()
+            to_owner(r).start()
+
+        @pl.when((s >= Y_LAG) & jnp.logical_not(by_y(s - Y_LAG)) & ((s - Y_LAG) % nx == nx - 1))
+        def _():
+            r = s - Y_LAG
+            m = r // (2 * nx)
+            v = s1[r].astype(f32)
+            for i in range(nx - 1):
+                along_x(r - nx + 1 + i).wait_recv()
+                v = v + x_in[m, i].astype(f32)
+            s3[m] = v.astype(bf16)
+            for q in range(ny):
+
+                @pl.when(jnp.logical_not(mine_at(r, q)))
+                def _():
+                    to_owner_y(r, q).start()
 
         @pl.when(s == P_STEP)
         def _():
@@ -296,30 +332,33 @@
             def _(k):
                 v = parts[x * nz + k]
                 for i in range(nx - 1):
-                    v = v + px_in[i, k]
-                psum[k] = v
+                    v = v + px_in[i, k].astype(f32)
+                psum[k] = v.astype(bf16)
 
             for i in range(nz - 1):
                 parts_z(i).start()
 
-    v = psum[z]
+    v = psum[z].astype(f32)
     for i in range(nz - 1):
         parts_z(i).wait_recv()
-        v = v + pz_in[i]
+        v = v + pz_in[i].astype(f32)
     pooled[...] = v / pick(tile)
 
     finals = [(tile, (slide + d) % sz.slides) for d in range(1, sz.slides)]
 
     @pl.when(is_owner)
     def _():
-        own[...] = s2[pairs - 1].astype(f32)
-
-        @pl.loop(1, sz.tiles)
+        own[...] = s3[nk // 2 - 1, y].astype(f32)
+
+        @pl.loop(0, sz.nz * nx)
         def _(d):
-            source = ((tile // 2) * 2 + sz.tiles - d) % sz.tiles
-            source = source + (d // (sz.tiles - 1)) * ((tile // 2) * 2 + 1 - z % 2 - source)
-            remote(s2.at[0], o_in.at[source], os.at[0], orr.at[source], mate).wait_recv()
-            own[...] += o_in[source].astype(f32)
+            from_z = 2 * ((z // 2 + nk - 1 - d // (2 * nx)) % nk) + (d // nx) % 2
+            i = d % nx
+
+            @pl.when(jnp.logical_not((from_z == z) & (i == y)))
+            def _():
+                remote(s2.at[0], o_in.at[from_z, i], os.at[0], orr.at[from_z, i], mate).wait_recv()
+                own[...] += o_in[from_z, i].astype(f32)
 
         final[...] = (own[...] / LOSS_SCALE).astype(bf16)
         for d, peer in enumerate(finals):
@@ -355,12 +394,24 @@
     @pl.loop(0, pairs)
     def _(s):
         swap(s).wait_send()
-        for i in range(ny - 1):
-            along_y(i, s).wait_send()
-
-        @pl.when(2 * pair_at(s) + c != tile)
-        def _():
+
+        @pl.when(by_y(s))
+        def _():
+            for i in range(ny - 1):
+                along_y(i, s).wait_send()
             to_owner(s).wait_send()
+
+        @pl.when(jnp.logical_not(by_y(s)) & (s % nx != nx - 1))
+        def _():
+            along_x(s).wait_send()
+
+        @pl.when(jnp.logical_not(by_y(s)) & (s % nx == nx - 1))
+        def _():
+            for q in range(ny):
+
+                @pl.when(jnp.logical_not(mine_at(s, q)))
+                def _():
+                    to_owner_y(s, q).wait_send()
 
 
 def shards(sz, tiles, counts, weights, slide_of, owner_map, cot, conv_weight):
@@ -397,18 +448,21 @@
             pltpu.VMEM((pairs, LANES, TAPS * LANES), bf16),
             pltpu.VMEM((pairs, ROWS, LANES), f32),
             pltpu.VMEM((sz.tiles, pairs, LANES), f32),
+            pltpu.VMEM((sz.tiles, pairs, LANES), bf16),
             pltpu.VMEM((2, pairs, sz.ny, pad, LANES), bf16),
             pltpu.VMEM((pairs, sz.ny, pad, LANES), bf16),
             pltpu.VMEM((pairs, sz.ny, pad, LANES), bf16),
             pltpu.VMEM((sz.ny - 1, pairs, pad, LANES), bf16),
             pltpu.VMEM((pairs, pad, LANES), bf16),
-            pltpu.VMEM((sz.tiles, pad, LANES), bf16),
+            pltpu.VMEM((sz.nz // 4, sz.nx - 1, sz.ny, pad, LANES), bf16),
+            pltpu.VMEM((sz.nz // 4, sz.ny, pad, LANES), bf16),
+            pltpu.VMEM((sz.nz, sz.nx, pad, LANES), bf16),
             pltpu.VMEM((pad, LANES), f32),
             pltpu.VMEM((pad, LANES), bf16),
             pltpu.VMEM((sz.ny, pad, LANES), bf16),
-            pltpu.VMEM((sz.nx - 1, sz.nz, pairs, LANES), f32),
-            pltpu.VMEM((sz.nz, pairs, LANES), f32),
-            pltpu.VMEM((sz.nz - 1, pairs, LANES), f32),
+            pltpu.VMEM((sz.nx - 1, sz.nz, pairs, LANES), bf16),
+            pltpu.VMEM((sz.nz, pairs, LANES), bf16),
+            pltpu.VMEM((sz.nz - 1, pairs, LANES), bf16),
         ]
         + [dma((pairs,))] * 2
         + [dma((sz.nz - 1,))] * 2
@@ -417,7 +471,9 @@
         + [dma((sz.nx - 1,))] * 2
         + [dma((pairs,))] * 2
         + [dma((sz.ny - 1, pairs))] * 2
-        + [dma((pairs,)), dma((sz.tiles,))]
+        + [dma((pairs,)), dma((sz.nz, sz.nx))]
+        + [dma((sz.nz // 4, sz.nx - 1))] * 2
+        + [dma((sz.nz // 4, sz.ny))]
         + [dma((sz.slides,)), dma((sz.ny,))]
         + [dma((sz.nx - 1,))] * 2
         + [dma((sz.nz - 1,))] * 2,

time: 59.9 us -> 57.8 us (0.965)
  Pallas kernels: 53.2 us -> 51.1 us
    pallas_call x1, Pallas kernels: 53.2 us -> 51.1 us  [shards(): pl.pallas_call(functools.partial(fused_kernel, sz), out_shape=(jax.ShapeD...]
where the time goes in v4:
time: 57.8 us; the launch traced here: 57.5 us
  Pallas kernels  51.1 us (88%)
  local copies, waits for them, and re-layouts  5.18 us (9%)
  between operations  1.29 us (2%)
    pallas_call x1, Pallas kernels, shards(): pl.pallas_call(functools.partial(fused_kernel, sz), out_shape=(jax.ShapeD...  51.1 us
    unnamed x5, local copies, waits for them, and re-layouts  5.18 us

profile of v4, /device:TPU:1, one launch (start us, length us, event | category | flops | bytes accessed | tf_op | source)
XLA Modules:
  0.0 57.5 jit_solution(11734738181931312304)
XLA Ops:
  1.3 51.1 %fused.1 = (f32[16,128]{1,0:T(8,128)}, f32[3,7,7,1,2048]{4,3,2,1,0:T(1,128)}, f32[9,64,64]{2,1,0:T(8,128)}) custom-call(s32[1,1]{1,0:T(1,128)S(6)} %copy.13.counts, f32[1,3]{1,0:T(1,128)} %weights.1, s32[1,3]{1,0:T(1,128)} %bitcast.5, s32[1,32]{1,0:T(1,128)} %owner_map.1, bf16[1,1,2048]{2,1,0:T(2,128)(2,1)} %cot.1, bf16[1,3,7,7,2048]{4,3,2,1,0:T(8,128)(2,1)} %tiles_hbm.1, ...), custom_call_target="tpu_custom_call" | custom-call | tf_op jit(solution)/shard_map/fused/pallas_call | solution.py:424
  52.3 1.3 %copy.14 = f32[1,1,2048]{2,1,0:T(1,128)} copy(f32[1,1,2048]{2,1,0:T(1,128)} %bitcast.4) | data formatting | bytes 16384
  53.6 0.0 copy-start
  53.6 3.2 %copy.15 = f32[1,3,7,7,2048]{4,0,3,2,1:T(1,128)} copy(f32[1,3,7,7,2048]{4,0,3,2,1:T(1,128)} %bitcast.3) | data formatting | bytes 2408448
  56.8 0.0 copy-done
  56.8 0.7 %copy.16 = f32[9,64,64]{2,1,0:T(8,128)} copy(f32[9,64,64]{2,1,0:T(8,128)S(1)} %copy-done) | data formatting | bytes 294912
Async XLA Ops:
  53.6 3.2 %copy-start = (f32[9,64,64]{2,1,0:T(8,128)S(1)}, f32[9,64,64]{2,1,0:T(8,128)}, u32[]{:S(2)}) copy-start(f32[9,64,64]{2,1,0:T(8,128)} %get-tuple-element.14) | copy-start | bytes 442372

commit v5 on v4

--- a/solution.py
+++ b/solution.py
@@ -55,12 +55,14 @@
     return coef, owner_map[0, slide_of[0, slot]]
 
 
-C_LAG = 4
-Y_LAG = 9
-X_LAG = 9
-BARRIER_STEP = 1
+C_LAG = 3
+Y_LAG = 12
+X_LAG = 3
+X_COUNT = 0
+X_MIDDLE = 12
+BARRIER_STEP = 0
 Z_STEP = 6
-P_STEP = 5
+P_STEP = 17
 
 
 def fused_kernel(
@@ -70,11 +72,12 @@
     xp, gp, xc, gc, w_rows, w_lanes, slopes, parts, parts16,
     terms, c_in, s1, y_in, s2, x_in, s3, o_in, own, final, fin, px_in, psum, pz_in,
     tile_sem, weight_sem, gzs, gzr, gxs, gxr, tzs, tzr, txs, txr,
-    cs, cr, ys, yr, os, orr, xs, xr, os3, fs, fr, pxs, pxr, pzs, pzr,
+    cs, cr, ys, yr, os, orr, xs, xr, os3, fs, fr, ms, mr, pxs, pxr, pzs, pzr,
 ):
     tile, slide, x, z, y, c = position(sz)
     nx, ny, nz, pairs = sz.nx, sz.ny, sz.nz, sz.pairs
     share, nk = sz.share, nz // 2
+    early, middle = min(X_COUNT, pairs), min(X_MIDDLE, pairs)
     z_peers = [(x * nz + (z + off) % nz, slide) for off in range(1, nz)]
     x_peers = [(((x + off) % nx) * nz + z, slide) for off in range(1, nx)]
     mate = (tile, y * 2 + 1 - c)
@@ -97,17 +100,10 @@
             pltpu.make_async_copy(weight_hbm.at[:, :, lanes], weight.at[s], weight_sem.at[s]),
         )
 
-    @pl.loop(0, pairs)
-    def _(s):
-        for copy in load(s):
-            copy.start()
-
     partners = z_peers + x_peers + y_peers + [mate]
     for peer in partners:
         signal(peer)
 
-    xp[...] = jnp.zeros_like(xp)
-    gp[...] = jnp.zeros_like(gp)
     for j in range(pairs):
         stage[pl.ds(j, 1), :] = cot[0, :, pl.ds(j * LANES, LANES)].astype(f32)
     all_cot[tile] = stage[...].astype(bf16)
@@ -117,6 +113,14 @@
     for coef, target in routes:
         mine = mine + jnp.where(lane == target, coef, 0.0)
     my_total[...] = mine
+
+    @pl.loop(0, pairs)
+    def _(s):
+        for copy in load(s):
+            copy.start()
+
+    xp[...] = jnp.zeros_like(xp)
+    gp[...] = jnp.zeros_like(gp)
 
     def total_z(i):
         return remote(my_total, z_total.at[i], tzs.at[i], tzr.at[i], z_peers[i])
@@ -244,6 +248,21 @@
         upstream = [grad[t, pl.ds(pair_at(s), 1), :] / (SIDE * SIDE) for t in range(SLOTS)]
         return [upstream[t] * slopes[s, pl.ds(64 * t, 64), :] for t in range(SLOTS)]
 
+    def input_gradient(r):
+        for t, rows in enumerate(pre_grad(r)):
+            gp[pl.ds(BASE + 64 * t, 64), :] = rows
+        for tap in range(TAPS):
+            shift = 8 * (tap // 3 - 1) + tap % 3 - 1
+            gc[:, pl.ds(tap * LANES, LANES)] = gp[pl.ds(BASE - shift, ROWS), :].astype(bf16)
+        dx = lax.dot_general(
+            gc[...], w_lanes[r], (((1,), (1,)), ((), ())), preferred_element_type=f32
+        )
+        lanes = lanes_of(r)
+        for t in range(SLOTS):
+            for h in range(SIDE):
+                at = 64 * t + 8 * h
+                input_grad[t, h, :, :, lanes] = dx[at : at + SIDE].reshape(SIDE, 1, LANES)
+
     @pl.loop(0, pairs + Y_LAG)
     def _(s):
         @pl.when(s < pairs)
@@ -266,22 +285,9 @@
                         terms[parity, s, yy, pl.ds(16 * j, 16), :] = jnp.concatenate(block, axis=0).astype(bf16)
             swap(s).start()
 
-        @pl.when((s >= X_LAG) & (s < pairs + X_LAG))
-        def _():
-            r = s - X_LAG
-            for t, rows in enumerate(pre_grad(r)):
-                gp[pl.ds(BASE + 64 * t, 64), :] = rows
-            for tap in range(TAPS):
-                shift = 8 * (tap // 3 - 1) + tap % 3 - 1
-                gc[:, pl.ds(tap * LANES, LANES)] = gp[pl.ds(BASE - shift, ROWS), :].astype(bf16)
-            dx = lax.dot_general(
-                gc[...], w_lanes[r], (((1,), (1,)), ((), ())), preferred_element_type=f32
-            )
-            lanes = lanes_of(r)
-            for t in range(SLOTS):
-                for h in range(SIDE):
-                    at = 64 * t + 8 * h
-                    input_grad[t, h, :, :, lanes] = dx[at : at + SIDE].reshape(SIDE, 1, LANES)
+        @pl.when((s >= X_LAG) & (s < early + X_LAG))
+        def _():
+            input_gradient(s - X_LAG)
 
         @pl.when((s >= C_LAG) & (s < pairs + C_LAG))
         def _():
@@ -323,7 +329,7 @@
                 def _():
                     to_owner_y(r, q).start()
 
-        @pl.when(s == P_STEP)
+        @pl.when(s == min(P_STEP, pairs + Y_LAG - 1))
         def _():
             for i in range(nx - 1):
                 parts_x(i).wait_recv()
@@ -338,13 +344,22 @@
             for i in range(nz - 1):
                 parts_z(i).start()
 
+    @pl.loop(early, middle)
+    def _(s):
+        input_gradient(s)
+
     v = psum[z].astype(f32)
     for i in range(nz - 1):
         parts_z(i).wait_recv()
         v = v + pz_in[i].astype(f32)
     pooled[...] = v / pick(tile)
 
-    finals = [(tile, (slide + d) % sz.slides) for d in range(1, sz.slides)]
+    def final_y(i):
+        return remote(final, fin.at[y], fs.at[i], fr.at[i], y_peers[i])
+
+    def final_mate(i):
+        piece = fin.at[(y + ny - i) % ny]
+        return remote(piece, piece, ms.at[i], mr.at[i], mate)
 
     @pl.when(is_owner)
     def _():
@@ -361,26 +376,14 @@
                 own[...] += o_in[from_z, i].astype(f32)
 
         final[...] = (own[...] / LOSS_SCALE).astype(bf16)
-        for d, peer in enumerate(finals):
-            remote(final, fin.at[y], fs.at[d], fr.at[y], peer).start()
+        for i in range(ny - 1):
+            final_y(i).start()
         fin[y] = final[...]
-
-    for q in range(ny):
-
-        @pl.when(jnp.logical_not(is_owner & (y == q)))
-        def _():
-            remote(final, fin.at[q], fs.at[0], fr.at[q], finals[0]).wait_recv()
-
-    every = [fin[q].astype(f32) for q in range(ny)]
-    for tap in range(TAPS):
-        rows = [v[tap * share : (tap + 1) * share] for v in every]
-        block = jnp.concatenate(rows, axis=0).T
-        result[tap] = jnp.concatenate([block[0:WIDTH], block[WIDTH:]], axis=1)
-
-    @pl.when(is_owner)
-    def _():
-        for d, peer in enumerate(finals):
-            remote(final, fin.at[y], fs.at[d], fr.at[y], peer).wait_send()
+        final_mate(0).start()
+
+    @pl.loop(middle, pairs)
+    def _(s):
+        input_gradient(s)
 
     for i in range(nz - 1):
         total_z(i).wait_send()
@@ -413,6 +416,42 @@
                 def _():
                     to_owner_y(s, q).wait_send()
 
+    @pl.when(is_owner)
+    def _():
+        for i in range(ny - 1):
+            piece = fin.at[(y + ny - 1 - i) % ny]
+            remote(final, piece, fs.at[i], fr.at[i], y_peers[i]).wait_recv()
+            final_mate(i + 1).start()
+
+    @pl.when(jnp.logical_not(is_owner))
+    def _():
+        for i in range(ny):
+            final_mate(i).wait_recv()
+
+    every = [fin[q].astype(f32) for q in range(ny)]
+    for tap in range(TAPS):
+        rows = [v[tap * share : (tap + 1) * share] for v in every]
+        block = jnp.concatenate(rows, axis=0).T
+        result[tap] = jnp.concatenate([block[0:WIDTH], block[WIDTH:]], axis=1)
+
+    @pl.when(is_owner)
+    def _():
+        for i in range(ny - 1):
+            final_y(i).wait_send()
+        for i in range(ny):
+            final_mate(i).wait_send()
+
+
+def finish_kernel(a, b, c, a_out, b_out, c_out, sems):
+    copies = [
+        pltpu.make_async_copy(src, dst, sems.at[i])
+        for i, (src, dst) in enumerate(((a, a_out), (b, b_out), (c, c_out)))
+    ]
+    for copy in copies:
+        copy.start()
+    for copy in copies:
+        copy.wait()
+
 
 def shards(sz, tiles, counts, weights, slide_of, owner_map, cot, conv_weight):
     pairs, channels = sz.pairs, sz.tiles * WIDTH
@@ -421,13 +460,14 @@
     hbm = pl.BlockSpec(memory_space=pltpu.MemorySpace.HBM)
     dma = pltpu.SemaphoreType.DMA
     pad = sz.packed_pad
-    pooled, input_grad, weight_grad = pl.pallas_call(
+    results = (
+        jax.ShapeDtypeStruct((pairs, LANES), f32),
+        jax.ShapeDtypeStruct((SLOTS, SIDE, SIDE, 1, channels), f32),
+        jax.ShapeDtypeStruct((TAPS, WIDTH, WIDTH), f32),
+    )
+    made = pl.pallas_call(
         functools.partial(fused_kernel, sz),
-        out_shape=(
-            jax.ShapeDtypeStruct((pairs, LANES), f32),
-            jax.ShapeDtypeStruct((SLOTS, SIDE, SIDE, 1, channels), f32),
-            jax.ShapeDtypeStruct((TAPS, WIDTH, WIDTH), f32),
-        ),
+        out_shape=tuple(pltpu.VMEM(r.shape, r.dtype) for r in results),
         in_specs=[smem] * 4 + [vmem] + [hbm] * 2,
         out_specs=(vmem, vmem, vmem),
         scratch_shapes=[
@@ -474,7 +514,8 @@
         + [dma((pairs,)), dma((sz.nz, sz.nx))]
         + [dma((sz.nz // 4, sz.nx - 1))] * 2
         + [dma((sz.nz // 4, sz.ny))]
-        + [dma((sz.slides,)), dma((sz.ny,))]
+        + [dma((sz.ny - 1,))] * 2
+        + [dma((sz.ny,))] * 2
         + [dma((sz.nx - 1,))] * 2
         + [dma((sz.nz - 1,))] * 2,
         compiler_params=pltpu.CompilerParams(
@@ -482,6 +523,14 @@
         ),
         name="fused",
     )(counts, weights, slide_of[:, :, 0], owner_map, cot, tiles, conv_weight)
+    pooled, input_grad, weight_grad = pl.pallas_call(
+        finish_kernel,
+        out_shape=results,
+        in_specs=[vmem] * 3,
+        out_specs=(hbm,) * 3,
+        scratch_shapes=[dma((3,))],
+        name="finish",
+    )(*[pltpu.with_memory_space_constraint(v, pltpu.MemorySpace.VMEM) for v in made])
     input_grad = input_grad.reshape(1, SLOTS, SIDE, SIDE, channels)
     return pooled.reshape(1, 1, channels), input_grad, weight_grad
 

time: 57.8 us -> 50.7 us (0.88)
  local copies, waits for them, and re-layouts: 5.18 us -> 0 us
  Pallas kernels: 51.1 us -> 48.7 us
    unnamed x5 -> x0, local copies, waits for them, and re-layouts: 5.18 us -> none
    pallas_call x1 -> x2, Pallas kernels: 51.1 us -> 48.7 us  [the longest x1 47.6 us: shards(): pl.pallas_call(functools.partial(fused_kernel, sz), out_shape=tuple((pltp...]
where the time goes in v5:
time: 50.7 us; the launch traced here: 50 us
  Pallas kernels  48.7 us (96%)
  between operations  1.29 us (3%)
    pallas_call x1, Pallas kernels, shards(): pl.pallas_call(functools.partial(fused_kernel, sz), out_shape=tuple((pltp...  47.6 us
    pallas_call x1, Pallas kernels, shards(): pl.pallas_call(finish_kernel, out_shape=results, in_specs=[vmem] * 3, out...  1.14 us

profile of v5, /device:TPU:1, one launch (start us, length us, event | category | flops | bytes accessed | tf_op | source)
XLA Modules:
  0.0 50.0 jit_solution(4745875399801712670)
XLA Ops:
  1.3 47.6 %fused.1 = (f32[16,128]{1,0:T(8,128)S(1)}, f32[3,7,7,1,2048]{4,3,2,1,0:T(1,128)S(1)}, f32[9,64,64]{2,1,0:T(8,128)S(1)}) custom-call(s32[1,1]{1,0:T(1,128)S(6)} %copy.10.counts, f32[1,3]{1,0:T(1,128)} %weights.1, s32[1,3]{1,0:T(1,128)} %bitcast.3, s32[1,32]{1,0:T(1,128)} %owner_map.1, bf16[1,1,2048]{2,1,0:T(2,128)(2,1)} %cot.1, ...), custom_call_target="tpu_custom_call" | custom-call | tf_op jit(solution)/shard_map/fused/pallas_call | solution.py:468
  48.8 1.1 %finish.1 = (f32[16,128]{1,0:T(8,128)}, f32[3,7,7,1,2048]{4,3,2,1,0:T(1,128)}, f32[9,64,64]{2,1,0:T(8,128)}) custom-call(f32[16,128]{1,0:T(8,128)S(1)} %get-tuple-element.9.a, f32[3,7,7,1,2048]{4,3,2,1,0:T(1,128)S(1)} %get-tuple-element.10.b, f32[9,64,64]{2,1,0:T(8,128)S(1)} %get-tuple-element.11.c), custom_call_target="tpu_custom_call" | custom-call | tf_op jit(solution)/shard_map/finish/pallas_call | solution.py:526

commit v6 on v5

--- a/solution.py
+++ b/solution.py
@@ -31,7 +31,6 @@
         self.pairs = self.tiles // 2
         self.share = 32 // self.ny
         self.packed = TAPS * self.share
-        self.packed_pad = (self.packed + 15) // 16 * 16
 
 
 def position(sz):
@@ -242,7 +241,6 @@
         return is_owner & (owner_k(s) == z // 2) & (q == y)
 
     low = lax.broadcasted_iota(jnp.int32, (32, LANES), 1) < WIDTH
-    none = jnp.zeros((share, LANES), f32)
 
     def pre_grad(s):
         upstream = [grad[t, pl.ds(pair_at(s), 1), :] / (SIDE * SIDE) for t in range(SLOTS)]
@@ -277,12 +275,10 @@
             per = 16 // share
             for parity, rows in enumerate((even, odd)):
                 for yy in range(ny):
-                    for j in range(sz.packed_pad // 16):
-                        block = [
-                            rows[tap][yy * share : (yy + 1) * share] if tap < TAPS else none
-                            for tap in range(j * per, (j + 1) * per)
-                        ]
-                        terms[parity, s, yy, pl.ds(16 * j, 16), :] = jnp.concatenate(block, axis=0).astype(bf16)
+                    for first in range(0, TAPS, per):
+                        block = [v[yy * share : (yy + 1) * share] for v in rows[first : first + per]]
+                        at = pl.ds(first * share, len(block) * share)
+                        terms[parity, s, yy, at, :] = jnp.concatenate(block, axis=0).astype(bf16)
             swap(s).start()
 
         @pl.when((s >= X_LAG) & (s < early + X_LAG))
@@ -459,7 +455,7 @@
     vmem = pl.BlockSpec(memory_space=pltpu.VMEM)
     hbm = pl.BlockSpec(memory_space=pltpu.MemorySpace.HBM)
     dma = pltpu.SemaphoreType.DMA
-    pad = sz.packed_pad
+    pad = sz.packed
     results = (
         jax.ShapeDtypeStruct((pairs, LANES), f32),
         jax.ShapeDtypeStruct((SLOTS, SIDE, SIDE, 1, channels), f32),

time: 50.7 us -> 49.6 us (0.978); the launches traced: 50 us -> 49.5 us
  no operation moved by 1% of the time
where the time goes in v6:
time: 49.6 us; the launch traced here: 49.5 us
  Pallas kernels  48.2 us (97%)
  between operations  1.29 us (3%)
    pallas_call x1, Pallas kernels, shards(): pl.pallas_call(functools.partial(fused_kernel, sz), out_shape=tuple((pltp...  47.1 us
    pallas_call x1, Pallas kernels, shards(): pl.pallas_call(finish_kernel, out_shape=results, in_specs=[vmem] * 3, out...  1.14 us

profile of v6, /device:TPU:1, one launch (start us, length us, event | category | flops | bytes accessed | tf_op | source)
XLA Modules:
  0.0 49.5 jit_solution(457401731216171832)
XLA Ops:
  1.3 47.1 %fused.1 = (f32[16,128]{1,0:T(8,128)S(1)}, f32[3,7,7,1,2048]{4,3,2,1,0:T(1,128)S(1)}, f32[9,64,64]{2,1,0:T(8,128)S(1)}) custom-call(s32[1,1]{1,0:T(1,128)S(6)} %copy.10.counts, f32[1,3]{1,0:T(1,128)} %weights.1, s32[1,3]{1,0:T(1,128)} %bitcast.3, s32[1,32]{1,0:T(1,128)} %owner_map.1, bf16[1,1,2048]{2,1,0:T(2,128)(2,1)} %cot.1, ...), custom_call_target="tpu_custom_call" | custom-call | tf_op jit(solution)/shard_map/fused/pallas_call | solution.py:464
  48.3 1.1 %finish.1 = (f32[16,128]{1,0:T(8,128)}, f32[3,7,7,1,2048]{4,3,2,1,0:T(1,128)}, f32[9,64,64]{2,1,0:T(8,128)}) custom-call(f32[16,128]{1,0:T(8,128)S(1)} %get-tuple-element.9.a, f32[3,7,7,1,2048]{4,3,2,1,0:T(1,128)S(1)} %get-tuple-element.10.b, f32[9,64,64]{2,1,0:T(8,128)S(1)} %get-tuple-element.11.c), custom_call_target="tpu_custom_call" | custom-call | tf_op jit(solution)/shard_map/finish/pallas_call | solution.py:522

commit v7 on v6

--- a/solution.py
+++ b/solution.py
@@ -60,8 +60,8 @@
 X_COUNT = 0
 X_MIDDLE = 12
 BARRIER_STEP = 0
-Z_STEP = 6
-P_STEP = 17
+Z_STEP = 8
+P_STEP = 20
 
 
 def fused_kernel(

time: 49.6 us -> 49.3 us (level)
  no operation moved by 1% of the time
where the time goes in v7:
time: 49.3 us; the launch traced here: 49.2 us
  Pallas kernels  47.9 us (97%)
  between operations  1.29 us (3%)
    pallas_call x1, Pallas kernels, shards(): pl.pallas_call(functools.partial(fused_kernel, sz), out_shape=tuple((pltp...  46.8 us
    pallas_call x1, Pallas kernels, shards(): pl.pallas_call(finish_kernel, out_shape=results, in_specs=[vmem] * 3, out...  1.14 us

profile of v7, /device:TPU:1, one launch (start us, length us, event | category | flops | bytes accessed | tf_op | source)
XLA Modules:
  0.0 49.2 jit_solution(5883494372745328222)
XLA Ops:
  1.3 46.8 %fused.1 = (f32[16,128]{1,0:T(8,128)S(1)}, f32[3,7,7,1,2048]{4,3,2,1,0:T(1,128)S(1)}, f32[9,64,64]{2,1,0:T(8,128)S(1)}) custom-call(s32[1,1]{1,0:T(1,128)S(6)} %copy.10.counts, f32[1,3]{1,0:T(1,128)} %weights.1, s32[1,3]{1,0:T(1,128)} %bitcast.3, s32[1,32]{1,0:T(1,128)} %owner_map.1, bf16[1,1,2048]{2,1,0:T(2,128)(2,1)} %cot.1, ...), custom_call_target="tpu_custom_call" | custom-call | tf_op jit(solution)/shard_map/fused/pallas_call | solution.py:464
  48.0 1.1 %finish.1 = (f32[16,128]{1,0:T(8,128)}, f32[3,7,7,1,2048]{4,3,2,1,0:T(1,128)}, f32[9,64,64]{2,1,0:T(8,128)}) custom-call(f32[16,128]{1,0:T(8,128)S(1)} %get-tuple-element.9.a, f32[3,7,7,1,2048]{4,3,2,1,0:T(1,128)S(1)} %get-tuple-element.10.b, f32[9,64,64]{2,1,0:T(8,128)S(1)} %get-tuple-element.11.c), custom_call_target="tpu_custom_call" | custom-call | tf_op jit(solution)/shard_map/finish/pallas_call | solution.py:522
